TPU v7x, 32 devices: a whole 2x2x4 slice. The times are simulated.
32 devices in a mesh: batch: 16 (over z, y, core), win: 2 (over x).
Axes of the slice: x: 2, y: 2, z: 4, core: 2. Of those that a mesh axis runs over, the one named last changes fastest.
Arguments:
- images: bfloat16 [64, 28, 28, 384], P('batch', 'win'), may hold values from -6 to 6
- valid_mask: int32 [64, 28, 28], P('batch', 'win'), may hold values 0 or 1
- cotangent: bfloat16 [64, 28, 28, 384], P('batch', 'win'), may hold values from -6 to 6
- conv_param: float32 [3, 10, 384], replicated, may hold values from -1.5 to 1.5
- norm_gain: float32 [4, 384], replicated, may hold values from 0.5 to 1.5
- norm_shift: float32 [4, 384], replicated, may hold values from -1 to 1
- qkv_weight: bfloat16 [2, 384, 1152], replicated, may hold values from -0.3125 to 0.3125
- attention_bias: float32 [7, 384], replicated, may hold values from -1 to 1
- out_weight: bfloat16 [2, 384, 384], replicated, may hold values from -1.25 to 1.25
- up_weight: bfloat16 [2, 384, 1536], replicated, may hold values from -0.3125 to 0.3125
- up_bias: float32 [2, 1536], replicated, may hold values from -1 to 1
- down_weight: bfloat16 [2, 1536, 384], replicated, may hold values from -0.15625 to 0.15625
- down_bias: float32 [2, 384], replicated, may hold values from -1 to 1
Outputs:
- output: float32 [64, 28, 28, 384], P('batch', 'win')
- images_grad: float32 [64, 28, 28, 384], P('batch', 'win')
- conv_grad: float32 [3, 10, 384], replicated
- gain_grad: float32 [4, 384], replicated
- shift_grad: float32 [4, 384], replicated
- qkv_grad: float32 [2, 384, 1152], replicated
- bias_grad: float32 [7, 384], replicated
- out_grad: float32 [2, 384, 384], replicated
- up_grad: float32 [2, 384, 1536], replicated
- up_bias_grad: float32 [2, 1536], replicated
- down_grad: float32 [2, 1536, 384], replicated
- down_bias_grad: float32 [2, 384], replicated
Inputs may be any that keep to these rules, and one draw needn't show every extreme that they name: `valid_mask`: 0 marks a patch left out of the channel-attention sums.
All inputs are finite; a program needn't handle non-finite values. No bound on the sum of `valid_mask` on one device may be relied on, other than what follows from the above.
Results may differ from a plain program's by a relative error of at most 0.017.
Values may be sent and summed in bfloat16 or wider, within the bound.
No kernel may reach another device: no remote copies, remote signals or barrier semaphores. Data moves between devices by JAX's collectives and lax.ppermute only.
A program may use at most 256 MiB of HBM per device.

v0:
```python
import jax
import jax.numpy as jnp
from jax import lax
from jax.sharding import PartitionSpec as P

D = 384
HEADS = 12
HD = 32
WIN = 7
SIDE = 28


epsilon = 1e-05


def extended(cells, sides, width):
    for axis, dim in sides:
        count = lax.axis_size(axis)
        ends = count - 1
        head = lax.slice_in_dim(cells, 0, width, axis=dim)
        tail = lax.slice_in_dim(cells, cells.shape[dim] - width, cells.shape[dim], axis=dim)
        cells = jnp.concatenate(
            [
                lax.ppermute(tail, axis, [(i, (i + 1) % count) for i in range(ends)]),
                cells,
                lax.ppermute(head, axis, [((i + 1) % count, i) for i in range(ends)]),
            ],
            axis=dim,
        )
    return cells


def layer_norm(volume, norm_gain, norm_shift):
    center = volume - jnp.mean(volume, axis=-1, keepdims=True)
    spread = jnp.mean(center * center, axis=-1, keepdims=True)
    return center * lax.rsqrt(spread + epsilon) * norm_gain + norm_shift


def exact_gelu(inputs):
    return jax.nn.gelu(inputs, approximate=False)


def position(volume, kernel):
    row_count, col_count = (volume.shape[1], volume.shape[2])
    padded = extended(volume, (("win", 1),), 1)
    padded = jnp.pad(padded, ((0, 0), (0, 0), (1, 1), (0, 0)))
    summed = volume + kernel[9]
    for tap_row in range(3):
        for tap_col in range(3):
            summed = (
                summed
                + padded[:, tap_row : tap_row + row_count, tap_col : tap_col + col_count, :]
                * kernel[3 * tap_row + tap_col]
            )
    return (summed, padded)


def position_back(gradient, padded, kernel):
    row_count, col_count = (gradient.shape[1], gradient.shape[2])
    grad_pad = extended(gradient, (("win", 1),), 1)
    grad_pad = jnp.pad(grad_pad, ((0, 0), (0, 0), (1, 1), (0, 0)))
    summed = gradient
    tap_grads = []
    for tap_row in range(3):
        for tap_col in range(3):
            summed = (
                summed
                + grad_pad[
                    :,
                    2 - tap_row : 2 - tap_row + row_count,
                    2 - tap_col : 2 - tap_col + col_count,
                    :,
                ]
                * kernel[3 * tap_row + tap_col]
            )
            tap_grads.append(
                jnp.sum(
                    gradient
                    * padded[:, tap_row : tap_row + row_count, tap_col : tap_col + col_count, :],
                    axis=(0, 1, 2),
                )
            )
    tap_grads.append(jnp.sum(gradient, axis=(0, 1, 2)))
    return (summed, jnp.stack(tap_grads))


def to_windows(volume):
    image_count, row_count, col_count, depth = volume.shape
    blocks = volume.reshape(image_count, row_count // WIN, WIN, col_count // WIN, WIN, depth)
    return blocks.transpose(0, 1, 3, 2, 4, 5).reshape(-1, WIN * WIN, depth)


def from_windows(blocks, image_count, row_count, col_count):
    depth = blocks.shape[-1]
    volume = blocks.reshape(image_count, row_count // WIN, col_count // WIN, WIN, WIN, depth)
    return volume.transpose(0, 1, 3, 2, 4, 5).reshape(image_count, row_count, col_count, depth)


def linear(inputs_b, weight, offset):
    return jnp.dot(inputs_b, weight, preferred_element_type=jnp.float32) + offset


def linear_back(inputs_b, weight, grad_b):
    grad_inputs = jnp.dot(grad_b, weight.T, preferred_element_type=jnp.float32)
    grad_weight = jnp.dot(inputs_b.T, grad_b, preferred_element_type=jnp.float32)
    grad_offset = jnp.sum(grad_b.astype(jnp.float32), axis=0)
    return (grad_inputs, grad_weight, grad_offset)


def window_forward(normed_b, weight, offset, out_matrix, out_offset):
    image_count, row_count, col_count = (normed_b.shape[0], normed_b.shape[1], normed_b.shape[2])
    flat_rows = normed_b.reshape(-1, D)
    joined = linear(flat_rows, weight, offset).astype(jnp.bfloat16)
    blocks = to_windows(joined.reshape(image_count, row_count, col_count, 3 * D))
    window_count = blocks.shape[0]
    queries = blocks[..., :D].reshape(window_count, WIN * WIN, HEADS, HD)
    key_rows = blocks[..., D : 2 * D].reshape(window_count, WIN * WIN, HEADS, HD)
    value_rows = blocks[..., 2 * D :].reshape(window_count, WIN * WIN, HEADS, HD)
    scores = jnp.einsum(
        "wqhc,wkhc->whqk", queries, key_rows, preferred_element_type=jnp.float32
    ) * HD ** (-0.5)
    attend = jax.nn.softmax(scores, axis=-1)
    attend_b = attend.astype(jnp.bfloat16)
    blended = jnp.einsum(
        "whqk,wkhc->wqhc", attend_b, value_rows, preferred_element_type=jnp.float32
    )
    blended = from_windows(
        blended.reshape(window_count, WIN * WIN, D), image_count, row_count, col_count
    )
    blended_b = blended.reshape(-1, D).astype(jnp.bfloat16)
    result = linear(blended_b, out_matrix, out_offset).reshape(normed_b.shape)
    return (result, (flat_rows, queries, key_rows, value_rows, attend, attend_b, blended_b))


def window_back(gradient, saved, weight, out_matrix):
    flat_rows, queries, key_rows, value_rows, attend, attend_b, blended_b = saved
    image_count, row_count, col_count = (gradient.shape[0], gradient.shape[1], gradient.shape[2])
    window_count = queries.shape[0]
    grad_b = gradient.reshape(-1, D).astype(jnp.bfloat16)
    grad_blended, grad_out_w, grad_out_b = linear_back(blended_b, out_matrix, grad_b)
    grad_blended_b = to_windows(
        grad_blended.astype(jnp.bfloat16).reshape(image_count, row_count, col_count, D)
    )
    grad_blended_b = grad_blended_b.reshape(window_count, WIN * WIN, HEADS, HD)
    grad_attend = jnp.einsum(
        "wqhc,wkhc->whqk", grad_blended_b, value_rows, preferred_element_type=jnp.float32
    )
    grad_values = jnp.einsum(
        "whqk,wqhc->wkhc", attend_b, grad_blended_b, preferred_element_type=jnp.float32
    )
    grad_scores = attend * (grad_attend - jnp.sum(grad_attend * attend, axis=-1, keepdims=True))
    grad_scores_b = grad_scores.astype(jnp.bfloat16)
    grad_queries = jnp.einsum(
        "whqk,wkhc->wqhc", grad_scores_b, key_rows, preferred_element_type=jnp.float32
    ) * HD ** (-0.5)
    grad_keys = jnp.einsum(
        "whqk,wqhc->wkhc", grad_scores_b, queries, preferred_element_type=jnp.float32
    ) * HD ** (-0.5)
    joined = jnp.concatenate(
        [
            grad_queries.reshape(window_count, WIN * WIN, D),
            grad_keys.reshape(window_count, WIN * WIN, D),
            grad_values.reshape(window_count, WIN * WIN, D),
        ],
        axis=-1,
    )
    grad_joined_b = (
        from_windows(joined, image_count, row_count, col_count)
        .reshape(-1, 3 * D)
        .astype(jnp.bfloat16)
    )
    grad_normed, grad_weight, grad_offset = linear_back(flat_rows, weight, grad_joined_b)
    return (grad_normed.reshape(gradient.shape), grad_weight, grad_offset, grad_out_w, grad_out_b)


def channel_forward(normed_b, mask_b, weight, offset, out_matrix, out_offset):
    image_count = normed_b.shape[0]
    flat_rows = normed_b.reshape(-1, D)
    joined = linear(flat_rows, weight, offset).astype(jnp.bfloat16).reshape(image_count, -1, 3 * D)
    queries = (joined[..., :D] * mask_b).reshape(image_count, -1, HEADS, HD)
    key_rows = joined[..., D : 2 * D].reshape(image_count, -1, HEADS, HD)
    value_rows = joined[..., 2 * D :].reshape(image_count, -1, HEADS, HD)
    partial_gram = jnp.einsum(
        "gnhi,gnhj->ghij", queries, key_rows, preferred_element_type=jnp.float32
    )
    gram = lax.psum(partial_gram, "win") / SIDE
    mixing = jax.nn.softmax(gram, axis=-1)
    mixing_b = mixing.astype(jnp.bfloat16)
    blended = jnp.einsum(
        "ghij,gnhj->gnhi", mixing_b, value_rows, preferred_element_type=jnp.float32
    )
    blended_b = blended.reshape(-1, D).astype(jnp.bfloat16)
    result = linear(blended_b, out_matrix, out_offset).reshape(normed_b.shape)
    return (result, (flat_rows, queries, key_rows, value_rows, mixing, mixing_b, blended_b))


def channel_back(gradient, saved, mask_col, weight, out_matrix):
    flat_rows, queries, key_rows, value_rows, mixing, mixing_b, blended_b = saved
    image_count = queries.shape[0]
    grad_b = gradient.reshape(-1, D).astype(jnp.bfloat16)
    grad_blended, grad_out_w, grad_out_b = linear_back(blended_b, out_matrix, grad_b)
    grad_blended_b = grad_blended.astype(jnp.bfloat16).reshape(image_count, -1, HEADS, HD)
    local_mixing = jnp.einsum(
        "gnhi,gnhj->ghij", grad_blended_b, value_rows, preferred_element_type=jnp.float32
    )
    grad_mixing = lax.psum(local_mixing, "win")
    grad_values = jnp.einsum(
        "ghij,gnhi->gnhj", mixing_b, grad_blended_b, preferred_element_type=jnp.float32
    )
    grad_gram = mixing * (grad_mixing - jnp.sum(grad_mixing * mixing, axis=-1, keepdims=True))
    grad_gram_b = grad_gram.astype(jnp.bfloat16)
    grad_queries = (
        jnp.einsum("ghij,gnhj->gnhi", grad_gram_b, key_rows, preferred_element_type=jnp.float32)
        / SIDE
    )
    grad_keys = (
        jnp.einsum("ghij,gnhi->gnhj", grad_gram_b, queries, preferred_element_type=jnp.float32)
        / SIDE
    )
    joined = jnp.concatenate(
        [
            grad_queries.reshape(image_count, -1, D) * mask_col,
            grad_keys.reshape(image_count, -1, D),
            grad_values.reshape(image_count, -1, D),
        ],
        axis=-1,
    )
    grad_joined_b = joined.reshape(-1, 3 * D).astype(jnp.bfloat16)
    grad_normed, grad_weight, grad_offset = linear_back(flat_rows, weight, grad_joined_b)
    return (grad_normed.reshape(gradient.shape), grad_weight, grad_offset, grad_out_w, grad_out_b)


def mlp_forward(normed_b, up_matrix, up_offset, down_matrix, down_offset):
    flat_rows = normed_b.reshape(-1, D)
    pre_act = linear(flat_rows, up_matrix, up_offset)
    hidden, hidden_pull = jax.vjp(exact_gelu, pre_act)
    hidden_b = hidden.astype(jnp.bfloat16)
    result = linear(hidden_b, down_matrix, down_offset).reshape(normed_b.shape)
    return (result, (flat_rows, hidden_pull, hidden_b))


def mlp_back(gradient, saved, up_matrix, down_matrix):
    flat_rows, hidden_pull, hidden_b = saved
    grad_b = gradient.reshape(-1, D).astype(jnp.bfloat16)
    grad_hidden, grad_down_w, grad_down_b = linear_back(hidden_b, down_matrix, grad_b)
    grad_pre_b = hidden_pull(grad_hidden)[0].astype(jnp.bfloat16)
    grad_normed, grad_up_w, grad_up_b = linear_back(flat_rows, up_matrix, grad_pre_b)
    return (grad_normed.reshape(gradient.shape), grad_up_w, grad_up_b, grad_down_w, grad_down_b)


def shards(
    images,
    valid_mask,
    cotangent,
    conv_param,
    norm_gain,
    norm_shift,
    qkv_weight,
    attention_bias,
    out_weight,
    up_weight,
    up_bias,
    down_weight,
    down_bias,
):
    image_count, row_count, col_count = (images.shape[0], images.shape[1], images.shape[2])
    mask_col = valid_mask.reshape(image_count, row_count * col_count, 1).astype(jnp.float32)
    mask_b = mask_col.astype(jnp.bfloat16)
    pos_one, padded_one = position(images.astype(jnp.float32), conv_param[0])
    normed_one, pull_one = jax.vjp(layer_norm, pos_one, norm_gain[0], norm_shift[0])
    window_offset = jnp.concatenate(
        [attention_bias[0], jnp.zeros((D,), jnp.float32), attention_bias[1]]
    )
    attn_one, saved_one = window_forward(
        normed_one.astype(jnp.bfloat16),
        qkv_weight[0],
        window_offset,
        out_weight[0],
        attention_bias[2],
    )
    resid_one = pos_one + attn_one
    pos_two, padded_two = position(resid_one, conv_param[1])
    normed_two, pull_two = jax.vjp(layer_norm, pos_two, norm_gain[1], norm_shift[1])
    mlp_one, saved_two = mlp_forward(
        normed_two.astype(jnp.bfloat16), up_weight[0], up_bias[0], down_weight[0], down_bias[0]
    )
    resid_two = pos_two + mlp_one
    pos_three, padded_three = position(resid_two, conv_param[2])
    normed_three, pull_three = jax.vjp(layer_norm, pos_three, norm_gain[2], norm_shift[2])
    attn_two, saved_three = channel_forward(
        normed_three.astype(jnp.bfloat16),
        mask_b,
        qkv_weight[1],
        attention_bias[3:6].reshape(-1),
        out_weight[1],
        attention_bias[6],
    )
    resid_three = pos_three + attn_two
    normed_four, pull_four = jax.vjp(layer_norm, resid_three, norm_gain[3], norm_shift[3])
    mlp_two, saved_four = mlp_forward(
        normed_four.astype(jnp.bfloat16), up_weight[1], up_bias[1], down_weight[1], down_bias[1]
    )
    output = resid_three + mlp_two
    grad_out = cotangent.astype(jnp.float32)
    grad_normed, grad_up_two, grad_upb_two, grad_down_two, grad_downb_two = mlp_back(
        grad_out, saved_four, up_weight[1], down_weight[1]
    )
    grad_resid, gain_four, shift_four = pull_four(grad_normed)
    grad_resid_three = grad_out + grad_resid
    grad_normed, grad_qkv_two, grad_bias_two, grad_outw_two, grad_outb_two = channel_back(
        grad_resid_three, saved_three, mask_col, qkv_weight[1], out_weight[1]
    )
    grad_pos, gain_three, shift_three = pull_three(grad_normed)
    grad_pos_three = grad_resid_three + grad_pos
    grad_resid_two, conv_three = position_back(grad_pos_three, padded_three, conv_param[2])
    late_conv = conv_three[None]
    late_gain = jnp.stack([gain_three, gain_four])
    late_shift = jnp.stack([shift_three, shift_four])
    late_bias = jnp.concatenate([grad_bias_two.reshape(3, D), grad_outb_two[None]], axis=0)
    grad_normed, grad_up_one, grad_upb_one, grad_down_one, grad_downb_one = mlp_back(
        grad_resid_two, saved_two, up_weight[0], down_weight[0]
    )
    grad_pos, gain_two, shift_two = pull_two(grad_normed)
    grad_pos_two = grad_resid_two + grad_pos
    grad_resid_one, conv_two = position_back(grad_pos_two, padded_two, conv_param[1])
    grad_normed, grad_qkv_one, grad_bias_one, grad_outw_one, grad_outb_one = window_back(
        grad_resid_one, saved_one, qkv_weight[0], out_weight[0]
    )
    grad_pos, gain_one, shift_one = pull_one(grad_normed)
    grad_pos_one = grad_resid_one + grad_pos
    images_grad, conv_one = position_back(grad_pos_one, padded_one, conv_param[0])
    early_conv = jnp.stack([conv_one, conv_two])
    early_gain = jnp.stack([gain_one, gain_two])
    early_shift = jnp.stack([shift_one, shift_two])
    early_bias = jnp.stack([grad_bias_one[:D], grad_bias_one[2 * D :], grad_outb_one])
    summed_all = lax.psum(
        (
            early_conv,
            early_gain,
            early_shift,
            grad_qkv_one,
            early_bias,
            grad_outw_one,
            grad_up_one,
            grad_upb_one,
            grad_down_one,
            grad_downb_one,
            late_conv,
            late_gain,
            late_shift,
            grad_qkv_two,
            late_bias,
            grad_outw_two,
            grad_up_two,
            grad_upb_two,
            grad_down_two,
            grad_downb_two,
        ),
        ("batch", "win"),
    )
    early_sum = summed_all[:10]
    late_sum = summed_all[10:]
    conv_grad = jnp.concatenate([early_sum[0], late_sum[0]], axis=0)
    gain_grad = jnp.concatenate([early_sum[1], late_sum[1]], axis=0)
    shift_grad = jnp.concatenate([early_sum[2], late_sum[2]], axis=0)
    qkv_grad = jnp.stack([early_sum[3], late_sum[3]])
    bias_grad = jnp.concatenate([early_sum[4], late_sum[4]], axis=0)
    out_grad = jnp.stack([early_sum[5], late_sum[5]])
    up_grad = jnp.stack([early_sum[6], late_sum[6]])
    up_bias_grad = jnp.stack([early_sum[7], late_sum[7]])
    down_grad = jnp.stack([early_sum[8], late_sum[8]])
    down_bias_grad = jnp.stack([early_sum[9], late_sum[9]])
    return (
        output,
        images_grad,
        conv_grad,
        gain_grad,
        shift_grad,
        qkv_grad,
        bias_grad,
        out_grad,
        up_grad,
        up_bias_grad,
        down_grad,
        down_bias_grad,
    )


def solution(mesh):
    in_specs = (
        P("batch", "win", None, None),
        P("batch", "win", None),
        P("batch", "win", None, None),
        P(),
        P(),
        P(),
        P(),
        P(),
        P(),
        P(),
        P(),
        P(),
        P(),
    )
    out_specs = (
        P("batch", "win", None, None),
        P("batch", "win", None, None),
        P(),
        P(),
        P(),
        P(),
        P(),
        P(),
        P(),
        P(),
        P(),
        P(),
    )
    return jax.shard_map(shards, mesh=mesh, in_specs=in_specs, out_specs=out_specs, check_vma=False)
```

profile of v0, /device:TPU:0, one launch (start us, length us, event | category | flops | bytes accessed | tf_op | source)
XLA Modules:
  0.0 1142.9 jit_solution(3478105498055559952)
XLA Ops:
  76.6 9.6 fusion.164
  86.2 8.5 convert_bitcast_fusion.1
  94.7 9.0 copy.52
  103.7 8.6 convert_element_type.191
  149.3 25.4 %multiply_convert_fusion.2 = (bf16[1568,1536]{1,0:T(8,128)(2,1)S(1)}, f32[1568,1536]{1,0:T(8,128)}, f32[1568,1536]{1,0:T(8,128)}) fusion(f32[1536]{0:T(1024)S(1)} %get-tuple-element.128, bf16[1568,384]{1,0:T(8,128)(2,1)} %reshape.406, bf16[2,384,1536]{2,1,0:T(8,128)(2,1)} %param.22), kind=kOutput, calls=%fused_computation.30 | convolution fusion | flops 2008645632 | bytes 26474496 | tf_op jit(solution)/shard_map/dot_general | solution.py:100
  233.8 25.5 %all-reduce.13.cloned.1.call-done = f32[4,12,32,32]{3,2,1,0:T(8,128)} async-done(((f32[4,12,32,32]{3,2,1,0:T(8,128)}), f32[4,12,32,32]{3,2,1,0:T(8,128)}) %all-reduce.13.cloned.1.call-update) | async-done | bytes 196624 | tf_op jit(solution)/shard_map/psum | solution.py:186
  287.1 24.7 %multiply_convert_fusion.1 = (bf16[1568,1536]{1,0:T(8,128)(2,1)}, f32[1568,1536]{1,0:T(8,128)S(1)}, f32[1568,1536]{1,0:T(8,128)}) fusion(f32[1536]{0:T(1024)S(1)} %copy-done.166, bf16[1568,384]{1,0:T(8,128)(2,1)S(1)} %reshape.414, bf16[2,384,1536]{2,1,0:T(8,128)(2,1)} %param.22), kind=kOutput, calls=%fused_computation.17 | convolution fusion | flops 2008645632 | bytes 26474496 | tf_op jit(solution)/shard_map/dot_general | solution.py:100
  311.9 8.1 convert_reduce_fusion
  325.9 8.2 dot_general.125
  334.1 8.0 multiply_reduce_fusion.2
  386.3 8.8 reshape.426
  400.9 7.9 copy.72
  411.8 20.8 %all-reduce.15.cloned.1.call-done = f32[4,12,32,32]{3,2,1,0:T(8,128)} async-done(((f32[4,12,32,32]{3,2,1,0:T(8,128)}), f32[4,12,32,32]{3,2,1,0:T(8,128)}) %all-reduce.15.cloned.1.call-update) | async-done | bytes 196624 | tf_op jit(solution)/shard_map/psum | solution.py:206
  460.5 10.2 reshape.425
  470.7 8.9 reshape.424
  479.6 7.8 copy.71
  487.4 7.9 copy.65
  540.0 10.6 convert_reduce_fusion.1
  550.6 8.2 dot_general.134
  595.1 8.2 reshape_reshape.14
  603.3 8.6 copy.74
  612.0 9.0 convert_bitcast_fusion
  620.9 8.4 multiply_reduce_fusion
  629.4 9.1 multiply_convert_fusion
  645.0 9.0 copy.81
  653.9 8.6 concatenate.121
  662.6 9.0 copy.76
  671.5 8.6 concatenate.119
  680.2 8.7 copy.78
  688.9 8.8 concatenate.120
  745.4 116.3 %all-reduce.17.cloned.1.call-done = (f32[1,10,384]{2,1,0:T(8,128)}, f32[2,10,384]{2,1,0:T(8,128)}, f32[2,384]{1,0:T(2,128)}, f32[2,384]{1,0:T(2,128)}, f32[2,384...) async-done(((f32[1,10,384]{2,1,0:T(8,128)}, ...) | async-done | bytes 84496 | tf_op jit(solution)/shard_map/psum | solution.py:336
  876.8 246.5 %all-reduce.19.cloned.1.call-done = (f32[1,384,1152]{2,1,0:T(8,128)}, f32[1,384,1152]{2,1,0:T(8,128)}, f32[1,384,384]{2,1,0:T(8,128)}, f32[1,384,384]{2,1,0:T(8,...) async-done(((f32[1,384,1152]{2,1,0:T(8,128)}, f32[1,384,1152]{2,1,0:T(8,128)}, ...) | async-done | bytes 14155792 | tf_op jit(solution)/shard_map/psum | solution.py:336
  (618 shorter events, 440.6 us)
Async XLA Ops:
  7.2 252.2 %all-reduce.13.cloned.1.call-start = ((), (), s32[]{:S(2)}) async-start(), calls=%async_computation | async-start | bytes 1572864 | tf_op jit(solution)/shard_map/psum | solution.py:186
  7.3 11.2 copy-start.161
  8.9 13.7 %copy-start.12 = (f32[4,14,28,384]{3,2,1,0:T(8,128)}, f32[4,14,28,384]{3,2,1,0:T(8,128)S(1)}, u32[]{:S(2)}) copy-start(f32[4,14,28,384]{3,2,1,0:T(8,128)S(1)} %copy_convert_fusion) | copy-start | bytes 7225348
  9.0 11.8 %collective-permute-start = (f32[4,1,28,384]{3,2,1,0:T(8,128)S(1)}, f32[4,1,28,384]{3,2,1,0:T(8,128)S(1)}, u32[]{:S(2)}, u32[]{:S(2)}) collective-permute-start(f32[4,1,28,384]{3,2,1,0:T(8,128)S(1)} %get-tuple-element.207), channel_id=1, source_target_pairs={{0,1},{2,3},{4,5},{6,7},{8,9},{10,11},{12,13},{14,15},{16,17},{18,... | collective-permute-start | bytes 516104 | tf_op jit(solution)/shard_map/ppermute | solution.py:24
  13.8 8.3 collective-permute-start.1
  17.9 12.4 %copy-start.94 = (f32[384]{0:T(512)}, f32[384]{0:T(512)S(1)}, u32[]{:S(2)}) copy-start(f32[384]{0:T(512)S(1)} %get-tuple-element.231) | copy-start | bytes 4612
  17.9 126.4 %copy-start.99 = (f32[384]{0:T(512)}, f32[384]{0:T(512)S(1)}, u32[]{:S(2)}) copy-start(f32[384]{0:T(512)S(1)} %get-tuple-element.232) | copy-start | bytes 4612
  20.7 118.9 %copy-start.123 = (f32[384]{0:T(512)}, f32[384]{0:T(512)S(1)}, u32[]{:S(2)}) copy-start(f32[384]{0:T(512)S(1)} %get-tuple-element.105) | copy-start | bytes 4612
  20.7 118.9 %copy-start.125 = (f32[384]{0:T(512)}, f32[384]{0:T(512)S(1)}, u32[]{:S(2)}) copy-start(f32[384]{0:T(512)S(1)} %get-tuple-element.106) | copy-start | bytes 4612
  28.7 96.9 %copy-start.6 = (f32[4,14,28,384]{3,2,1,0:T(8,128)}, f32[4,14,28,384]{3,2,1,0:T(8,128)S(1)}, u32[]{:S(2)}) copy-start(f32[4,14,28,384]{3,2,1,0:T(8,128)S(1)} %get-tuple-element.189) | copy-start | bytes 7225348
  127.9 11.7 %copy-start.14 = (f32[4,14,28,384]{3,2,1,0:T(8,128)}, f32[4,14,28,384]{3,2,1,0:T(8,128)S(1)}, u32[]{:S(2)}) copy-start(f32[4,14,28,384]{3,2,1,0:T(8,128)S(1)} %add.451) | copy-start | bytes 7225348
  128.0 6.9 collective-permute-start.2
  131.3 7.7 collective-permute-start.3
  142.7 41.6 %copy-start.8 = (f32[4,14,28,384]{3,2,1,0:T(8,128)}, f32[4,14,28,384]{3,2,1,0:T(8,128)S(1)}, u32[]{:S(2)}) copy-start(f32[4,14,28,384]{3,2,1,0:T(8,128)S(1)} %get-tuple-element.187) | copy-start | bytes 7225348
  149.3 27.5 %copy-start.177 = (bf16[2,1536,384]{2,1,0:T(8,128)(2,1)S(1)}, bf16[2,1536,384]{2,1,0:T(8,128)(2,1)}, u32[]{:S(2)}) copy-start(bf16[2,1536,384]{2,1,0:T(8,128)(2,1)} %param.24) | copy-start | bytes 7077892
  188.2 4.6 collective-permute-start.4
  189.7 7.6 collective-permute-start.5
  203.7 78.7 %copy-start.10 = (f32[4,14,28,384]{3,2,1,0:T(8,128)}, f32[4,14,28,384]{3,2,1,0:T(8,128)S(1)}, u32[]{:S(2)}) copy-start(f32[4,14,28,384]{3,2,1,0:T(8,128)S(1)} %get-tuple-element.183) | copy-start | bytes 7225348
  224.6 208.0 %all-reduce.15.cloned.1.call-start = ((), (), s32[]{:S(2)}) async-start(), calls=%async_computation.1 | async-start | bytes 1572864 | tf_op jit(solution)/shard_map/psum | solution.py:206
  287.1 24.7 %copy-start.67 = (bf16[1568,384]{1,0:T(8,128)(2,1)S(1)}, bf16[1568,384]{1,0:T(8,128)(2,1)}, u32[]{:S(2)}) copy-start(bf16[1568,384]{1,0:T(8,128)(2,1)} %convert_element_type.208) | copy-start | bytes 3612676
  287.1 24.7 %copy-start.178 = (bf16[2,1536,384]{2,1,0:T(8,128)(2,1)S(1)}, bf16[2,1536,384]{2,1,0:T(8,128)(2,1)}, u32[]{:S(2)}) copy-start(bf16[2,1536,384]{2,1,0:T(8,128)(2,1)} %param.24) | copy-start | bytes 7077892
  398.1 463.6 %all-reduce.17.cloned.1.call-start = ((), (), s32[]{:S(2)}) async-start(), calls=%async_computation.2 | async-start | bytes 227328 | tf_op jit(solution)/shard_map/psum | solution.py:336
  408.8 27.7 %copy-start.26 = (bf16[4,392,384]{1,2,0:T(8,128)(2,1)S(1)}, bf16[4,392,384]{1,2,0:T(8,128)(2,1)}, u32[]{:S(2)}) copy-start(bf16[4,392,384]{1,2,0:T(8,128)(2,1)} %copy.56) | copy-start | bytes 3612676
  504.7 13.5 %copy-start.174 = (f32[1,384]{1,0:T(1,128)S(1)}, f32[1,384]{1,0:T(1,128)}, u32[]{:S(2)}) copy-start(f32[1,384]{1,0:T(1,128)} %stack.256) | copy-start | bytes 4612
  514.7 9.4 collective-permute-start.6
  517.0 8.4 collective-permute-start.7
  564.6 11.2 slice-start
  571.2 9.9 collective-permute-start.8
  574.5 7.9 collective-permute-start.9
  732.3 391.0 %all-reduce.19.cloned.1.call-start = ((), (), s32[]{:S(2)}) async-start(), calls=%async_computation.3 | async-start | bytes 28311552 | tf_op jit(solution)/shard_map/psum | solution.py:336
  740.7 129.0 %collective-permute-start.10 = (f32[4,1,28,384]{3,2,1,0:T(8,128)S(1)}, f32[4,1,28,384]{3,2,1,0:T(8,128)S(1)}, u32[]{:S(2)}, u32[]{:S(2)}) collective-permute-start(f32[4,1,28,384]{3,2,1,0:T(8,128)S(1)} %get-tuple-element.196), channel_id=1, source_target_pairs={{0,1},{2,3},{4,5},{6,7},{8,9},{10,11},{12,13},{14,15},{16,17},{18,... | collective-permute-start | bytes 516104 | tf_op jit(solution)/shard_map/ppermute | solution.py:24
  744.1 125.6 %collective-permute-start.11 = (f32[4,1,28,384]{3,2,1,0:T(8,128)S(1)}, f32[4,1,28,384]{3,2,1,0:T(8,128)S(1)}, u32[]{:S(2)}, u32[]{:S(2)}) collective-permute-start(f32[4,1,28,384]{3,2,1,0:T(8,128)S(1)} %get-tuple-element.197), channel_id=1, source_target_pairs={{1,0},{3,2},{5,4},{7,6},{9,8},{11,10},{13,12},{15,14},{17,16},{19,... | collective-permute-start | bytes 516104 | tf_op jit(solution)/shard_map/ppermute | solution.py:26
  (169 other events, 722.6 us)
Sparse Core Ops, SparseCore 0:
  224.7 34.6 all-reduce.12
  398.2 34.3 all-reduce.14
  732.4 129.2 all-reduce.16
  869.7 253.5 all-reduce.18
where the time goes:
time: 1160 us; the launch traced here: 1140 us
  waiting for transfers between devices  424 us (37%)
  local copies, waits for them, and re-layouts  338 us (29%)
  matrix products  217 us (19%)
  other arithmetic  121 us (10%)
  starting transfers between devices  26.7 us (2%)
  between operations  16.7 us (1%)
    psum x2, waiting for transfers between devices, shards(): lax.psum((early_conv, early_gain, early_shift, grad_qkv_one, early_bias,...  363 us
    dot_general x8, matrix products, linear(): jnp.dot(inputs_b, weight, preferred_element_type=jnp.float32) + offset  77.1 us
    dot_general x8, matrix products, linear_back(): grad_inputs = jnp.dot(grad_b, weight.T, preferred_element_type=jnp.float32)  44.3 us
    concatenate x6, local copies, waits for them, and re-layouts, channel_back(): jnp.concatenate([grad_queries.reshape(image_count, -1, D) * mask_col, gra...  41.7 us
    dot_general x8, matrix products, linear_back(): jnp.dot(inputs_b.T, grad_b, preferred_element_type=jnp.float32)  36.5 us
    unnamed x374, local copies, waits for them, and re-layouts  33.2 us
    concatenate x3, local copies, waits for them, and re-layouts, window_back(): jnp.concatenate([grad_queries.reshape(window_count, WIN * WIN, D), grad_k...  26.1 us
    psum x1, waiting for transfers between devices, channel_forward(): gram = lax.psum(partial_gram, 'win') / SIDE  25.5 us
  transfers between devices with their start and end apart: 16, of which 11 were waited for; matrix products, arithmetic and copies ran while one was open for 6% of the time, Pallas kernels for 0%

commit v1 on v0

v1 whole, which is shorter than its diff:
```python
import functools

import jax
import jax.numpy as jnp
import numpy as np
from jax import lax
from jax.experimental import pallas as pl
from jax.experimental.pallas import tpu as pltpu
from jax.sharding import PartitionSpec as P

D = 384
HEADS = 12
HD = 32
FF = 1536
WIN = 7
COLS = 28
WIDE = 32
SLOT = 64
GROUPS = 3
LANES = 128
SIDE = 28
CHUNK = 256
EPS = 1e-05
SCALE = HD ** (-0.5)
F32 = jnp.float32
BF16 = jnp.bfloat16

STRIP = WIN * WIDE
WROWS = 4 * SLOT


def constants():
    perm = np.zeros((WROWS, STRIP), np.float32)
    for window in range(4):
        for r in range(WIN):
            for c in range(WIN):
                perm[window * SLOT + r * WIN + c, r * WIDE + window * WIN + c] = 1.0
    heads_window = np.zeros((4 * SLOT, LANES), np.float32)
    heads_channel = np.zeros((LANES, LANES), np.float32)
    for head in range(4):
        heads_window[head * SLOT : (head + 1) * SLOT, head * HD : (head + 1) * HD] = 1.0
        heads_channel[head * HD : (head + 1) * HD, head * HD : (head + 1) * HD] = 1.0
    return (
        jnp.asarray(perm, BF16),
        jnp.asarray(perm.T, BF16),
        jnp.asarray(heads_window, BF16),
        jnp.asarray(heads_channel, BF16),
    )


def dot(left, right):
    return jnp.dot(left, right, preferred_element_type=F32)


def dot_nt(left, right):
    return lax.dot_general(left, right, (((1,), (1,)), ((), ())), preferred_element_type=F32)


def dot_tn(left, right):
    return lax.dot_general(left, right, (((0,), (0,)), ((), ())), preferred_element_type=F32)


def normalized(z):
    center = z - jnp.sum(z, axis=-1, keepdims=True) * (1.0 / D)
    spread = jnp.sum(center * center, axis=-1, keepdims=True) * (1.0 / D)
    scale = lax.rsqrt(spread + EPS)
    return center * scale, scale


def normalized_back(grad, z, gain):
    xhat, scale = normalized(z)
    scaled = grad * gain
    mean_one = jnp.sum(scaled, axis=-1, keepdims=True) * (1.0 / D)
    mean_two = jnp.sum(scaled * xhat, axis=-1, keepdims=True) * (1.0 / D)
    return (scaled - mean_one - xhat * mean_two) * scale, grad * xhat


TAIL = 0.39 * 0.5**0.5
ERFC = tuple(
    0.5 * c
    for c in (
        0.2353252479818039,
        0.091388231495776,
        0.6495598567387839,
        -0.6354008448449706,
        0.886664715384384,
        -0.2275372084398586,
    )
)


def gelu_pair(x):
    bell = jnp.exp(x * x * -0.5)
    t = 1.0 / (1.0 + TAIL * jnp.abs(x))
    poly = ERFC[5] * t + ERFC[4]
    for c in (ERFC[3], ERFC[2], ERFC[1], ERFC[0]):
        poly = poly * t + c
    tail = poly * t * bell
    below = jnp.where(x >= 0, 1.0 - tail, tail)
    return x * below, below + x * bell * ((2.0 * np.pi) ** -0.5)


def column_mask(rows):
    return lax.broadcasted_iota(jnp.int32, (rows, 1), 0) % WIDE < COLS


def folded(block):
    return jnp.sum(block.reshape(block.shape[0] // 8, 8, block.shape[1]), axis=0)


def conv_row(ext, row, kernel):
    above, here, below = ext[row], ext[row + 1], ext[row + 2]
    left = kernel[0] * above + kernel[3] * here + kernel[6] * below
    center = kernel[1] * above + (1.0 + kernel[4]) * here + kernel[7] * below + kernel[9]
    right = kernel[2] * above + kernel[5] * here + kernel[8] * below
    return center + pltpu.roll(left, 1, 0) + pltpu.roll(right, WIDE - 1, 0)


def conv_row_back(ext, row, kernel):
    above, here, below = ext[row], ext[row + 1], ext[row + 2]
    left = kernel[0] * below + kernel[3] * here + kernel[6] * above
    center = kernel[1] * below + (1.0 + kernel[4]) * here + kernel[7] * above
    right = kernel[2] * below + kernel[5] * here + kernel[8] * above
    return center + pltpu.roll(left, WIDE - 1, 0) + pltpu.roll(right, 1, 0)


def tap_sums(z, ext, row, taps_ref):
    shifted = (pltpu.roll(z, 1, 0), z, pltpu.roll(z, WIDE - 1, 0))
    for a in range(3):
        grad = ext[row + 2 - a]
        for b in range(3):
            taps_ref[3 * a + b] += folded(shifted[b] * grad)
    taps_ref[9] += folded(ext[row + 1])


def taps(ref, layer):
    return [ref[layer, j : j + 1, :] for j in range(10)]


def put_halo(ext, side, halo, rows):
    ext[0] = jnp.where(side == 1, halo, 0.0)
    ext[rows + 1] = jnp.where(side == 0, halo, 0.0)


def put_border(border_ref, side, first, last):
    border_ref[0] = jnp.where(side == 0, last, first)


def first_step():
    return pl.program_id(0) == 0


def last_step():
    return pl.program_id(0) == pl.num_programs(0) - 1


def clear(*refs):
    @pl.when(first_step())
    def _():
        for ref in refs:
            ref[...] = jnp.zeros_like(ref)


def column_sum(block):
    return jnp.sum(block.astype(F32), axis=0, keepdims=True)


def pack_tiles(out_ref, start, value):
    rows = value.shape[0]
    for j in range(value.shape[1] // LANES):
        out_ref[start + j * rows : start + (j + 1) * rows, :] = value[:, j * LANES : (j + 1) * LANES].astype(BF16)


def window_scores(q, k, heads, group):
    lanes = slice(group * LANES, (group + 1) * LANES)
    spread_q = jnp.concatenate([q[:, lanes]] * 4, axis=0) * heads
    return dot_nt(k[:, lanes], spread_q), spread_q


def per_head(block, heads):
    kept = block * heads
    return kept[:SLOT] + kept[SLOT : 2 * SLOT] + kept[2 * SLOT : 3 * SLOT] + kept[3 * SLOT :]


def stage_one(side_ref, img_ref, halo_ref, conv_ref, gain_ref, shift_ref, qkv_w, bias_ref, out_w, perm_ref, back_ref, heads_ref,
              pos_ref, nw_ref, qkv_ref, att_ref, mix_ref, res_ref, border_ref, ext, nrm):
    rows = img_ref.shape[1]
    side = side_ref[0]
    load_image(img_ref, halo_ref, side, ext)
    kernel = taps(conv_ref, 0)
    gain, shift = gain_ref[0:1, :], shift_ref[0:1, :]

    @pl.loop(0, rows)
    def _(r):
        z = conv_row(ext, r, kernel)
        pos_ref[0, r] = z
        xhat, _ = normalized(z)
        nrm[pl.ds(pl.multiple_of(r * WIDE, WIDE), WIDE), :] = (xhat * gain + shift).astype(BF16)

    heads = heads_ref[...]
    heads_f = heads.astype(F32)
    real = lax.broadcasted_iota(jnp.int32, (SLOT, 1), 0) < WIN * WIN
    mask = column_mask(STRIP)

    @pl.loop(0, rows // WIN)
    def _(s):
        image_rows = pl.ds(pl.multiple_of(s * STRIP, STRIP), STRIP)
        window_rows = pl.ds(pl.multiple_of(s * WROWS, WROWS), WROWS)
        nw = dot(perm_ref[...], nrm[image_rows, :]).astype(BF16)
        nw_ref[0, window_rows, :] = nw
        for part in range(3):
            cols = slice(part * D, (part + 1) * D)
            value = dot(nw, qkv_w[0, :, cols])
            if part != 1:
                value = value + bias_ref[part // 2 : part // 2 + 1, :]
            qkv_ref[0, window_rows, cols] = value.astype(BF16)
        for window in range(4):
            slot = pl.ds(pl.multiple_of(s * WROWS + window * SLOT, SLOT), SLOT)
            q, k, v = (qkv_ref[0, slot, part * D : (part + 1) * D] for part in range(3))
            for group in range(GROUPS):
                scores, _ = window_scores(q, k, heads, group)
                scores = jnp.where(real, scores * SCALE, -1e30)
                raised = jnp.exp(scores - jnp.max(scores, axis=0, keepdims=True))
                attend = raised * (1.0 / jnp.sum(raised, axis=0, keepdims=True))
                att_ref[0, slot, group * WROWS : (group + 1) * WROWS] = attend
                lanes = slice(group * LANES, (group + 1) * LANES)
                mixed = per_head(dot_tn(attend.astype(BF16), v[:, lanes]), heads_f)
                mix_ref[0, slot, lanes] = mixed.astype(BF16)
        mixed = dot(back_ref[...], mix_ref[0, window_rows, :]).astype(BF16)
        attn = (dot(mixed, out_w[0]) + bias_ref[2:3, :]).reshape(WIN, WIDE, D)
        strip = pl.ds(s * WIN, WIN)
        value = (pos_ref[0, strip] + attn).reshape(STRIP, D)
        res_ref[0, strip] = jnp.where(mask, value, 0.0).reshape(WIN, WIDE, D)

    put_border(border_ref, side, res_ref[0, 0], res_ref[0, rows - 1])


def load_image(img_ref, halo_ref, side, ext):
    rows = img_ref.shape[1]
    ext[...] = jnp.zeros_like(ext)

    @pl.loop(0, rows)
    def _(r):
        ext[r + 1, :COLS, :] = img_ref[0, r].astype(F32)

    halo = halo_ref[0].astype(F32)
    ext[0, :COLS, :] = jnp.where(side == 1, halo, 0.0)
    ext[rows + 1, :COLS, :] = jnp.where(side == 0, halo, 0.0)


def load_rows(x_ref, halo_ref, side, ext):
    rows = x_ref.shape[1]

    @pl.loop(0, rows)
    def _(r):
        ext[r + 1] = x_ref[0, r]

    put_halo(ext, side, halo_ref[0], rows)


def stage_two(side_ref, x_ref, halo_ref, conv_ref, gain_ref, shift_ref, up_w, upb_ref, down_w, downb_ref,
              pos_ref, nrm_ref, hid_ref, der_ref, res_ref, border_ref, ext):
    rows = x_ref.shape[1]
    side = side_ref[0]
    load_rows(x_ref, halo_ref, side, ext)
    kernel = taps(conv_ref, 1)
    gain, shift = gain_ref[1:2, :], shift_ref[1:2, :]

    @pl.loop(0, rows)
    def _(r):
        z = conv_row(ext, r, kernel)
        pos_ref[0, r] = z
        xhat, _ = normalized(z)
        nrm_ref[0, pl.ds(pl.multiple_of(r * WIDE, WIDE), WIDE), :] = (xhat * gain + shift).astype(BF16)

    mask = column_mask(STRIP)

    @pl.loop(0, rows // WIN)
    def _(s):
        part = pl.ds(pl.multiple_of(s * STRIP, STRIP), STRIP)
        nrm = nrm_ref[0, part, :]
        for c in range(FF // CHUNK):
            cols = slice(c * CHUNK, (c + 1) * CHUNK)
            hidden, slope = gelu_pair(dot(nrm, up_w[0, :, cols]) + upb_ref[0:1, cols])
            hid_ref[0, part, cols] = hidden.astype(BF16)
            der_ref[0, part, cols] = slope.astype(BF16)
        out = (dot(hid_ref[0, part, :], down_w[0]) + downb_ref[0:1, :]).reshape(WIN, WIDE, D)
        strip = pl.ds(s * WIN, WIN)
        value = (pos_ref[0, strip] + out).reshape(STRIP, D)
        res_ref[0, strip] = jnp.where(mask, value, 0.0).reshape(WIN, WIDE, D)

    put_border(border_ref, side, res_ref[0, 0], res_ref[0, rows - 1])


def gram_fold(left, right, heads_f):
    full = dot_tn(left, right) * heads_f
    return full[:HD] + full[HD : 2 * HD] + full[2 * HD : 3 * HD] + full[3 * HD :]


def stage_three(side_ref, x_ref, halo_ref, conv_ref, gain_ref, shift_ref, qkv_w, bias_ref, valid_ref, heads_ref,
                pos_ref, nrm_ref, qkv_ref, gram_ref, ext):
    rows = x_ref.shape[1]
    load_rows(x_ref, halo_ref, side_ref[0], ext)
    kernel = taps(conv_ref, 2)
    gain, shift = gain_ref[2:3, :], shift_ref[2:3, :]

    @pl.loop(0, rows)
    def _(r):
        z = conv_row(ext, r, kernel)
        pos_ref[0, r] = z
        xhat, _ = normalized(z)
        nrm_ref[0, pl.ds(pl.multiple_of(r * WIDE, WIDE), WIDE), :] = (xhat * gain + shift).astype(BF16)

    @pl.loop(0, rows // WIN)
    def _(s):
        part = pl.ds(pl.multiple_of(s * STRIP, STRIP), STRIP)
        nrm = nrm_ref[0, part, :]
        valid = valid_ref[0, part, :]
        for third in range(3):
            cols = slice(third * D, (third + 1) * D)
            value = (dot(nrm, qkv_w[0, :, cols]) + bias_ref[3 + third : 4 + third, :]).astype(BF16)
            if third == 0:
                value = (value.astype(F32) * valid).astype(BF16)
            qkv_ref[0, part, cols] = value

    heads_f = heads_ref[...].astype(F32)
    for group in range(GROUPS):
        low = group * LANES
        gram_ref[0, group * HD : (group + 1) * HD, :] = gram_fold(
            qkv_ref[0, :, D + low : D + low + LANES], qkv_ref[0, :, low : low + LANES], heads_f
        )


def channel_weights(gram):
    gram = gram * (1.0 / SIDE)
    raised = jnp.exp(gram - jnp.max(gram, axis=0, keepdims=True))
    return raised / jnp.sum(raised, axis=0, keepdims=True)


def block_diagonal(block, heads):
    return jnp.concatenate([block.astype(BF16)] * 4, axis=0) * heads


def stage_four(pos_ref, qkv_ref, gram_a, gram_b, cot_ref, out_w, bias_ref, gain_ref, shift_ref, up_w, upb_ref, down_w, downb_ref,
               heads_ref,
               out_ref, gres_ref, gm_ref, gchan_ref, pack_ref, small_ref,
               mix, cotf, cotb, res, nrm, hid, gpre, gn, gb, up_acc, down_acc, out_acc, sums):
    rows = pos_ref.shape[1]
    clear(up_acc, down_acc, out_acc, sums)
    heads = heads_ref[...]
    for group in range(GROUPS):
        low = group * LANES
        gram_rows = slice(group * HD, (group + 1) * HD)
        chan = block_diagonal(channel_weights(gram_a[0, gram_rows] + gram_b[0, gram_rows]), heads)
        mix[:, low : low + LANES] = dot(qkv_ref[0, :, 2 * D + low : 2 * D + low + LANES], chan).astype(BF16)

    cotf[...] = jnp.zeros_like(cotf)

    @pl.loop(0, rows)
    def _(r):
        cotf[r, :COLS, :] = cot_ref[0, r].astype(F32)
        cotb[pl.ds(pl.multiple_of(r * WIDE, WIDE), WIDE), :] = cotf[r].astype(BF16)

    gain, shift = gain_ref[3:4, :], shift_ref[3:4, :]

    @pl.loop(0, rows // WIN)
    def _(s):
        part = pl.ds(pl.multiple_of(s * STRIP, STRIP), STRIP)
        strip = pl.ds(s * WIN, WIN)
        attn = (dot(mix[part, :], out_w[0]) + bias_ref[6:7, :]).reshape(WIN, WIDE, D)
        res[strip] = pos_ref[0, strip] + attn

    @pl.loop(0, rows)
    def _(r):
        xhat, _ = normalized(res[r])
        nrm[pl.ds(pl.multiple_of(r * WIDE, WIDE), WIDE), :] = (xhat * gain + shift).astype(BF16)

    @pl.loop(0, rows // WIN)
    def _(s):
        part = pl.ds(pl.multiple_of(s * STRIP, STRIP), STRIP)
        strip = pl.ds(s * WIN, WIN)
        normed, cot = nrm[part, :], cotb[part, :]
        for c in range(FF // CHUNK):
            cols = slice(c * CHUNK, (c + 1) * CHUNK)
            hidden, slope = gelu_pair(dot(normed, up_w[0, :, cols]) + upb_ref[1:2, cols])
            hid[part, cols] = hidden.astype(BF16)
            grad = (slope * dot_nt(cot, down_w[0, cols, :])).astype(BF16)
            gpre[part, cols] = grad
            sums[:, cols] += folded(grad.astype(F32))
        value = (dot(hid[part, :], down_w[0]) + downb_ref[1:2, :]).reshape(WIN, WIDE, D) + res[strip]
        out_ref[0, strip] = value[:, :COLS, :]
        gn[strip] = dot_nt(gpre[part, :], up_w[0]).reshape(WIN, WIDE, D)

    @pl.loop(0, rows)
    def _(r):
        grad = gn[r]
        back, gain_term = normalized_back(grad, res[r], gain)
        cot = cotf[r]
        total = cot + back
        gres_ref[0, r] = total
        low = total.astype(BF16)
        gb[pl.ds(pl.multiple_of(r * WIDE, WIDE), WIDE), :] = low
        sums[:, FF : FF + D] += folded(cot)
        sums[:, FF + D : FF + 2 * D] += folded(gain_term)
        sums[:, FF + 2 * D : FF + 3 * D] += folded(grad)
        sums[:, FF + 3 * D : FF + 4 * D] += folded(low.astype(F32))

    up_acc[...] += dot_tn(nrm[...], gpre[...])
    down_acc[...] += dot_tn(cotb[...], hid[...])
    out_acc[...] += dot_tn(mix[...], gb[...])
    gm = dot_nt(gb[...], out_w[0]).astype(BF16)
    gm_ref[0] = gm
    heads_f = heads.astype(F32)
    for group in range(GROUPS):
        low = group * LANES
        gchan_ref[0, group * HD : (group + 1) * HD, :] = gram_fold(
            qkv_ref[0, :, 2 * D + low : 2 * D + low + LANES], gm[:, low : low + LANES], heads_f
        )

    @pl.when(last_step())
    def _():
        pack_tiles(pack_ref, 0, up_acc[...])
        pack_tiles(pack_ref, FF // LANES * D, down_acc[...].T)
        pack_tiles(pack_ref, 2 * FF // LANES * D, out_acc[...])
        for j in range(FF // D + 4):
            small_ref[j : j + 1, :] = jnp.sum(sums[:, j * D : (j + 1) * D], axis=0, keepdims=True)


def stage_five(side_ref, gres_ref, pos_ref, nrm_ref, qkv_ref, gm_ref, gram_a, gram_b, gchan_a, gchan_b, valid_ref, qkv_w, gain_ref,
               heads_ref,
               gpos_ref, border_ref, pack_ref, small_ref,
               joined, gn, qkv_acc, sums):
    rows = pos_ref.shape[1]
    clear(qkv_acc, sums)
    heads = heads_ref[...]
    valid = valid_ref[0]
    for group in range(GROUPS):
        low = group * LANES
        gram_rows = slice(group * HD, (group + 1) * HD)
        chan = channel_weights(gram_a[0, gram_rows] + gram_b[0, gram_rows])
        grad_chan = gchan_a[0, gram_rows] + gchan_b[0, gram_rows]
        grad_gram = chan * (grad_chan - jnp.sum(grad_chan * chan, axis=0, keepdims=True))
        chan, grad_gram = block_diagonal(chan, heads), block_diagonal(grad_gram, heads)
        lanes = slice(low, low + LANES)
        q, k = qkv_ref[0, :, lanes], qkv_ref[0, :, D + low : D + low + LANES]
        joined[:, lanes] = (dot(k, grad_gram) * (1.0 / SIDE) * valid).astype(BF16)
        joined[:, D + low : D + low + LANES] = (dot_nt(q, grad_gram) * (1.0 / SIDE)).astype(BF16)
        joined[:, 2 * D + low : 2 * D + low + LANES] = dot_nt(gm_ref[0, :, lanes], chan).astype(BF16)
    for third in range(3):
        cols = slice(third * D, (third + 1) * D)
        block = joined[:, cols]
        sums[:, cols] += folded(block.astype(F32))
        qkv_acc[:, cols] += dot_tn(nrm_ref[0], block)
    gn[...] = dot_nt(joined[...], qkv_w[0]).reshape(gn.shape)
    gain = gain_ref[2:3, :]

    @pl.loop(0, rows)
    def _(r):
        grad = gn[r]
        back, gain_term = normalized_back(grad, pos_ref[0, r], gain)
        gpos_ref[0, r] = gres_ref[0, r] + back
        sums[:, 3 * D : 4 * D] += folded(gain_term)
        sums[:, 4 * D : 5 * D] += folded(grad)

    put_border(border_ref, side_ref[0], gpos_ref[0, 0], gpos_ref[0, rows - 1])

    @pl.when(last_step())
    def _():
        pack_tiles(pack_ref, 0, qkv_acc[...])
        for j in range(5):
            small_ref[j : j + 1, :] = jnp.sum(sums[:, j * D : (j + 1) * D], axis=0, keepdims=True)


def stage_six(side_ref, g_ref, halo_ref, x_ref, pos_ref, nrm_ref, hid_ref, der_ref, conv_ref, gain_ref, up_w, down_w,
              gpos_ref, border_ref, pack_ref, small_ref,
              ext, gres, gb, gpre, gn, up_acc, down_acc, sums, tap_acc):
    rows = pos_ref.shape[1]
    clear(up_acc, down_acc, sums, tap_acc)
    load_rows(g_ref, halo_ref, side_ref[0], ext)
    kernel = taps(conv_ref, 2)
    mask = column_mask(WIDE)

    @pl.loop(0, rows)
    def _(r):
        back = jnp.where(mask, conv_row_back(ext, r, kernel), 0.0)
        gres[r] = back
        low = back.astype(BF16)
        gb[pl.ds(pl.multiple_of(r * WIDE, WIDE), WIDE), :] = low
        sums[:, FF : FF + D] += folded(low.astype(F32))
        tap_sums(x_ref[0, r], ext, r, tap_acc)

    @pl.loop(0, rows // WIN)
    def _(s):
        part = pl.ds(pl.multiple_of(s * STRIP, STRIP), STRIP)
        grad = gb[part, :]
        for c in range(FF // CHUNK):
            cols = slice(c * CHUNK, (c + 1) * CHUNK)
            block = (der_ref[0, part, cols].astype(F32) * dot_nt(grad, down_w[0, cols, :])).astype(BF16)
            gpre[part, cols] = block
            sums[:, cols] += folded(block.astype(F32))
        gn[pl.ds(s * WIN, WIN)] = dot_nt(gpre[part, :], up_w[0]).reshape(WIN, WIDE, D)

    gain = gain_ref[1:2, :]

    @pl.loop(0, rows)
    def _(r):
        grad = gn[r]
        back, gain_term = normalized_back(grad, pos_ref[0, r], gain)
        gpos_ref[0, r] = gres[r] + back
        sums[:, FF + D : FF + 2 * D] += folded(gain_term)
        sums[:, FF + 2 * D : FF + 3 * D] += folded(grad)

    put_border(border_ref, side_ref[0], gpos_ref[0, 0], gpos_ref[0, rows - 1])
    up_acc[...] += dot_tn(nrm_ref[0], gpre[...])
    down_acc[...] += dot_tn(gb[...], hid_ref[0])

    @pl.when(last_step())
    def _():
        pack_tiles(pack_ref, 0, up_acc[...])
        pack_tiles(pack_ref, FF // LANES * D, down_acc[...].T)
        for j in range(FF // D + 3):
            small_ref[j : j + 1, :] = jnp.sum(sums[:, j * D : (j + 1) * D], axis=0, keepdims=True)
        for j in range(10):
            small_ref[8 + j : 9 + j, :] = jnp.sum(tap_acc[j], axis=0, keepdims=True)


def stage_seven(side_ref, g_ref, halo_ref, x_ref, pos_ref, img_ref, imghalo_ref, nw_ref, qkv_ref, att_ref, mix_ref, conv_ref,
                gain_ref, qkv_w, out_w, perm_ref, back_ref, heads_ref,
                gpos_ref, border_ref, pack_ref, small_ref,
                ext, gres, gb, joined, gn, qkv_acc, out_acc, sums, tap_acc, tap_one):
    rows = pos_ref.shape[1]
    side = side_ref[0]
    clear(qkv_acc, out_acc, sums, tap_acc, tap_one)
    load_rows(g_ref, halo_ref, side, ext)
    kernel = taps(conv_ref, 1)
    mask = column_mask(WIDE)

    @pl.loop(0, rows)
    def _(r):
        back = jnp.where(mask, conv_row_back(ext, r, kernel), 0.0)
        gres[r] = back
        low = back.astype(BF16)
        gb[pl.ds(pl.multiple_of(r * WIDE, WIDE), WIDE), :] = low
        sums[:, 3 * D : 4 * D] += folded(low.astype(F32))
        tap_sums(x_ref[0, r], ext, r, tap_acc)

    heads = heads_ref[...]
    heads_f = heads.astype(F32)

    @pl.loop(0, rows // WIN)
    def _(s):
        image_rows = pl.ds(pl.multiple_of(s * STRIP, STRIP), STRIP)
        window_rows = pl.ds(pl.multiple_of(s * WROWS, WROWS), WROWS)
        gbw = dot(perm_ref[...], gb[image_rows, :]).astype(BF16)
        out_acc[...] += dot_tn(mix_ref[0, window_rows, :], gbw)
        gm_all = dot_nt(gbw, out_w[0]).astype(BF16)
        for window in range(4):
            slot = pl.ds(pl.multiple_of(s * WROWS + window * SLOT, SLOT), SLOT)
            gm = gm_all[window * SLOT : (window + 1) * SLOT]
            q, k, v = (qkv_ref[0, slot, part * D : (part + 1) * D] for part in range(3))
            out_rows = slice(window * SLOT, (window + 1) * SLOT)
            for group in range(GROUPS):
                lanes = slice(group * LANES, (group + 1) * LANES)
                attend = att_ref[0, slot, group * WROWS : (group + 1) * WROWS]
                grad_att, spread_gm = window_scores(gm, v, heads, group)
                spread_q = jnp.concatenate([q[:, lanes]] * 4, axis=0) * heads
                weighted = grad_att * attend
                grad_s = (weighted - attend * jnp.sum(weighted, axis=0, keepdims=True)).astype(BF16)
                gv = dot(attend.astype(BF16), spread_gm)
                gk = dot(grad_s, spread_q) * SCALE
                gq = per_head(dot_tn(grad_s, k[:, lanes]), heads_f) * SCALE
                low = group * LANES
                joined[out_rows, low : low + LANES] = gq.astype(BF16)
                joined[out_rows, D + low : D + low + LANES] = gk.astype(BF16)
                joined[out_rows, 2 * D + low : 2 * D + low + LANES] = gv.astype(BF16)
        nw = nw_ref[0, window_rows, :]
        for third in range(3):
            cols = slice(third * D, (third + 1) * D)
            block = joined[:, cols]
            qkv_acc[:, cols] += dot_tn(nw, block)
            if third != 1:
                sums[:, cols] += folded(block.astype(F32))
        unwound = dot(back_ref[...], joined[...]).astype(BF16)
        gn[pl.ds(s * WIN, WIN)] = dot_nt(unwound, qkv_w[0]).reshape(WIN, WIDE, D)

    gain = gain_ref[0:1, :]

    @pl.loop(0, rows)
    def _(r):
        grad = gn[r]
        back, gain_term = normalized_back(grad, pos_ref[0, r], gain)
        gpos_ref[0, r] = gres[r] + back
        sums[:, D : 2 * D] += folded(gain_term)
        sums[:, 4 * D : 5 * D] += folded(grad)

    put_border(border_ref, side, gpos_ref[0, 0], gpos_ref[0, rows - 1])
    load_image(img_ref, imghalo_ref, side, ext)

    @pl.loop(0, rows)
    def _(r):
        grad = gpos_ref[0, r]
        shifted = (pltpu.roll(grad, WIDE - 1, 0), grad, pltpu.roll(grad, 1, 0))
        for a in range(3):
            z = ext[r + a]
            for b in range(3):
                tap_one[3 * a + b] += folded(shifted[b] * z)
        tap_one[9] += folded(grad)

    @pl.when(last_step())
    def _():
        pack_tiles(pack_ref, 0, qkv_acc[...])
        pack_tiles(pack_ref, 3 * D // LANES * D, out_acc[...])
        for j in range(5):
            small_ref[j : j + 1, :] = jnp.sum(sums[:, j * D : (j + 1) * D], axis=0, keepdims=True)
        for j in range(10):
            small_ref[8 + j : 9 + j, :] = jnp.sum(tap_acc[j], axis=0, keepdims=True)
            small_ref[18 + j : 19 + j, :] = jnp.sum(tap_one[j], axis=0, keepdims=True)


def stage_eight(side_ref, g_ref, halo_ref, conv_ref, out_ref, ext):
    rows = g_ref.shape[1]
    load_rows(g_ref, halo_ref, side_ref[0], ext)
    kernel = taps(conv_ref, 0)

    @pl.loop(0, rows)
    def _(r):
        out_ref[0, r] = conv_row_back(ext, r, kernel)[:COLS]


VMEM_LIMIT = 60 * 1024 * 1024


def per_image(shape):
    return pl.BlockSpec((1,) + tuple(shape[1:]), lambda i: (i,) + (0,) * (len(shape) - 1))


def whole(shape):
    return pl.BlockSpec(tuple(shape), lambda i: (0,) * len(shape))


def layer(array, index):
    shape = array.shape
    return pl.BlockSpec((1,) + tuple(shape[1:]), lambda i: (index,) + (0,) * (len(shape) - 1))


def scalar():
    return pl.BlockSpec(memory_space=pltpu.SMEM)


def call(body, images, in_specs, outs, scratch, flops, name):
    return pl.pallas_call(
        body,
        name=name,
        grid=(images,),
        in_specs=in_specs,
        out_specs=[per_image(shape) if own else whole(shape) for shape, _, own in outs],
        out_shape=[jax.ShapeDtypeStruct(shape, dtype) for shape, dtype, _ in outs],
        scratch_shapes=scratch,
        compiler_params=pltpu.CompilerParams(dimension_semantics=("arbitrary",), vmem_limit_bytes=VMEM_LIMIT),
        cost_estimate=pl.CostEstimate(flops=flops, bytes_accessed=20_000_000, transcendentals=0),
    )


def exchange(array):
    return lax.ppermute(array, "win", [(0, 1), (1, 0)])


def shards(images, valid_mask, cotangent, conv, gain, shift, qkv_w, bias, out_w, up_w, up_b, down_w, down_b):
    n, rows = images.shape[0], images.shape[1]
    side = lax.axis_index("win")
    side_arr = side.astype(jnp.int32).reshape(1)
    perm, back, heads_w, heads_c = constants()
    wide = (n, rows, WIDE, D)
    flat = rows * WIDE
    wflat = rows // WIN * WROWS
    border = (n, WIDE, D)
    valid = jnp.pad(valid_mask.astype(F32), ((0, 0), (0, 0), (0, WIDE - COLS))).reshape(n, flat, 1)
    ext = pltpu.VMEM((rows + 2, WIDE, D), F32)

    def vm(shape, dtype=F32):
        return pltpu.VMEM(shape, dtype)

    edge = jnp.where(side == 0, images[:, rows - 1], images[:, 0])
    img_halo = exchange(edge)
    small_params = [whole(conv.shape), whole(gain.shape)]

    pos_one, nw, qkv_one, att, mix_one, res_one, edge = call(
        stage_one, n,
        [scalar(), per_image(images.shape), per_image(img_halo.shape), *small_params, whole(shift.shape), layer(qkv_w, 0),
         whole(bias.shape), layer(out_w, 0), whole(perm.shape), whole(back.shape), whole(heads_w.shape)],
        [(wide, F32, True), ((n, wflat, D), BF16, True), ((n, wflat, 3 * D), BF16, True), ((n, wflat, GROUPS * WROWS), F32, True),
         ((n, wflat, D), BF16, True), (wide, F32, True), (border, F32, True)],
        [ext, vm((flat, D), BF16)], 2_000_000_000, "window_forward",
    )(side_arr, images, img_halo, conv, gain, shift, qkv_w, bias, out_w, perm, back, heads_w)

    halo = exchange(edge)
    pos_two, nrm_two, hid_one, der_one, res_two, edge = call(
        stage_two, n,
        [scalar(), per_image(wide), per_image(border), *small_params, whole(shift.shape), layer(up_w, 0), whole(up_b.shape),
         layer(down_w, 0), whole(down_b.shape)],
        [(wide, F32, True), ((n, flat, D), BF16, True), ((n, flat, FF), BF16, True), ((n, flat, FF), BF16, True), (wide, F32, True),
         (border, F32, True)],
        [ext], 4_000_000_000, "mlp_one_forward",
    )(side_arr, res_one, halo, conv, gain, shift, up_w, up_b, down_w, down_b)

    halo = exchange(edge)
    gram_shape = (n, GROUPS * HD, LANES)
    pos_three, nrm_three, qkv_two, gram = call(
        stage_three, n,
        [scalar(), per_image(wide), per_image(border), *small_params, whole(shift.shape), layer(qkv_w, 1), whole(bias.shape),
         per_image(valid.shape), whole(heads_c.shape)],
        [(wide, F32, True), ((n, flat, D), BF16, True), ((n, flat, 3 * D), BF16, True), (gram_shape, F32, True)],
        [ext], 2_000_000_000, "channel_gram",
    )(side_arr, res_two, halo, conv, gain, shift, qkv_w, bias, valid, heads_c)

    gram_other = exchange(gram)
    mlp_rows = 2 * FF // LANES * D
    out_rows = D // LANES * D
    qkv_rows = 3 * D // LANES * D
    output, gres_three, gm_two, gchan, pack_four, small_four = call(
        stage_four, n,
        [per_image(wide), per_image(qkv_two.shape), per_image(gram_shape), per_image(gram_shape), per_image(cotangent.shape),
         layer(out_w, 1), whole(bias.shape), whole(gain.shape), whole(shift.shape), layer(up_w, 1), whole(up_b.shape),
         layer(down_w, 1), whole(down_b.shape), whole(heads_c.shape)],
        [(images.shape, F32, True), (wide, F32, True), ((n, flat, D), BF16, True), (gram_shape, F32, True),
         ((mlp_rows + out_rows, LANES), BF16, False), ((8, D), F32, False)],
        [vm((flat, D), BF16), vm((rows, WIDE, D)), vm((flat, D), BF16), vm((rows, WIDE, D)), vm((flat, D), BF16),
         vm((flat, FF), BF16), vm((flat, FF), BF16), vm((rows, WIDE, D)), vm((flat, D), BF16),
         vm((D, FF)), vm((D, FF)), vm((D, D)), vm((8, FF + 4 * D))],
        12_000_000_000, "mlp_two",
    )(pos_three, qkv_two, gram, gram_other, cotangent, out_w, bias, gain, shift, up_w, up_b, down_w, down_b, heads_c)

    gchan_other = exchange(gchan)
    gpos_three, edge, pack_five, small_five = call(
        stage_five, n,
        [scalar(), per_image(wide), per_image(wide), per_image(nrm_three.shape), per_image(qkv_two.shape), per_image(gm_two.shape),
         per_image(gram_shape), per_image(gram_shape), per_image(gram_shape), per_image(gram_shape), per_image(valid.shape),
         layer(qkv_w, 1), whole(gain.shape), whole(heads_c.shape)],
        [(wide, F32, True), (border, F32, True), ((qkv_rows, LANES), BF16, False), ((8, D), F32, False)],
        [vm((flat, 3 * D), BF16), vm((rows, WIDE, D)), vm((D, 3 * D)), vm((8, 5 * D))], 3_000_000_000, "channel_backward",
    )(side_arr, gres_three, pos_three, nrm_three, qkv_two, gm_two, gram, gram_other, gchan, gchan_other, valid, qkv_w, gain,
      heads_c)

    halo = exchange(edge)
    gpos_two, edge, pack_six, small_six = call(
        stage_six, n,
        [scalar(), per_image(wide), per_image(border), per_image(wide), per_image(wide), per_image(nrm_two.shape),
         per_image(hid_one.shape), per_image(der_one.shape), *small_params, layer(up_w, 0), layer(down_w, 0)],
        [(wide, F32, True), (border, F32, True), ((mlp_rows, LANES), BF16, False), ((24, D), F32, False)],
        [ext, vm((rows, WIDE, D)), vm((flat, D), BF16), vm((flat, FF), BF16), vm((rows, WIDE, D)), vm((D, FF)), vm((D, FF)),
         vm((8, FF + 3 * D)), vm((10, 8, D))], 8_000_000_000, "mlp_one_backward",
    )(side_arr, gpos_three, halo, res_two, pos_two, nrm_two, hid_one, der_one, conv, gain, up_w, down_w)

    halo = exchange(edge)
    gpos_one, edge, pack_seven, small_seven = call(
        stage_seven, n,
        [scalar(), per_image(wide), per_image(border), per_image(wide), per_image(wide), per_image(images.shape),
         per_image(img_halo.shape), per_image(nw.shape), per_image(qkv_one.shape), per_image(att.shape), per_image(mix_one.shape),
         *small_params, layer(qkv_w, 0), layer(out_w, 0), whole(perm.shape), whole(back.shape), whole(heads_w.shape)],
        [(wide, F32, True), (border, F32, True), ((qkv_rows + out_rows, LANES), BF16, False), ((32, D), F32, False)],
        [ext, vm((rows, WIDE, D)), vm((flat, D), BF16), vm((WROWS, 3 * D), BF16), vm((rows, WIDE, D)), vm((D, 3 * D)), vm((D, D)),
         vm((8, 5 * D)), vm((10, 8, D)), vm((10, 8, D))], 5_000_000_000, "window_backward",
    )(side_arr, gpos_two, halo, res_one, pos_one, images, img_halo, nw, qkv_one, att, mix_one, conv, gain, qkv_w, out_w, perm, back,
      heads_w)

    halo = exchange(edge)
    (images_grad,) = call(
        stage_eight, n, [scalar(), per_image(wide), per_image(border), whole(conv.shape)], [(images.shape, F32, True)], [ext],
        10_000_000, "images_backward",
    )(side_arr, gpos_one, halo, conv)

    small = jnp.concatenate([small_four, small_five, small_six, small_seven], axis=0)
    small = jnp.pad(small.reshape(-1, LANES), ((0, SMALL_ROWS - 3 * 72), (0, 0))).astype(BF16)
    joined = jnp.concatenate([pack_four, pack_five, pack_six, pack_seven, small], axis=0)
    summed = all_sum(joined)
    return (output, images_grad, *unpack(summed))


SMALL_ROWS = 512


def steps_of(batch):
    bits = list(range((batch // 2).bit_length() - 1))
    one = ["w", *bits]
    two = [*bits[:1], "w", *bits[1:]]
    return list(zip(one, two))


def flip(place, win, axis):
    if axis == "w":
        return place, 1 - win
    return place ^ (2 << axis), win


def all_sum(x):
    batch = lax.axis_size("batch")
    place, win = lax.axis_index("batch"), lax.axis_index("win")
    core = place % 2

    def trade(value, axes):
        pairs = []
        for b in range(batch):
            for w in range(2):
                axis = axes[b % 2]
                to = (b ^ 1, w) if axis == "c" else flip(b, w, axis)
                pairs.append((2 * b + w, 2 * to[0] + to[1]))
        return lax.ppermute(value, ("batch", "win"), pairs)

    def bit(axis):
        if axis == "c":
            return core
        return win if axis == "w" else (place // (2 << axis)) % 2

    order = [("c", "c"), *steps_of(batch)]
    bits = [jnp.where(core == 0, bit(one), bit(two)) for one, two in order]
    for axes, mine in zip(order, bits):
        half = x.shape[0] // 2
        sent = lax.dynamic_slice_in_dim(x, (1 - mine) * half, half, 0)
        kept = lax.dynamic_slice_in_dim(x, mine * half, half, 0)
        got = trade(sent, axes)
        x = (kept.astype(F32) + got.astype(F32)).astype(BF16)
    for axes, mine in zip(order[::-1], bits[::-1]):
        got = trade(x, axes)
        x = jnp.concatenate([jnp.where(mine == 0, x, got), jnp.where(mine == 0, got, x)], axis=0)
    return x


def untile(x, start, height, width):
    n = width // LANES
    block = lax.slice_in_dim(x, start, start + n * height, axis=0).reshape(n, height, LANES)
    return block.transpose(1, 0, 2).reshape(height, width).astype(F32)


def unpack(x):
    mlp, out, qkv = 2 * FF // LANES * D, D // LANES * D, 3 * D // LANES * D
    up = FF // LANES * D
    at_five = mlp + out
    at_six = at_five + qkv
    at_seven = at_six + mlp
    at_small = at_seven + qkv + out
    up_grad = jnp.stack([untile(x, at_six, D, FF), untile(x, 0, D, FF)])
    down_grad = jnp.stack([untile(x, at_six + up, FF, D), untile(x, up, FF, D)])
    out_grad = jnp.stack([untile(x, at_seven + qkv, D, D), untile(x, mlp, D, D)])
    qkv_grad = jnp.stack([untile(x, at_seven, D, 3 * D), untile(x, at_five, D, 3 * D)])
    small = x[at_small : at_small + 216].reshape(72, D).astype(F32)
    four, five, six, seven = small[:8], small[8:16], small[16:40], small[40:72]
    conv_grad = jnp.stack([seven[18:28], seven[8:18], six[8:18]])
    gain_grad = jnp.stack([seven[1], six[5], five[3], four[5]])
    shift_grad = jnp.stack([seven[4], six[6], five[4], four[6]])
    bias_grad = jnp.stack([seven[0], seven[2], seven[3], five[0], five[1], five[2], four[7]])
    up_bias_grad = jnp.stack([six[:4].reshape(FF), four[:4].reshape(FF)])
    down_bias_grad = jnp.stack([six[4], four[4]])
    return (conv_grad, gain_grad, shift_grad, qkv_grad, bias_grad, out_grad, up_grad, up_bias_grad, down_grad, down_bias_grad)


def solution(mesh):
    split = P("batch", "win", None, None)
    in_specs = (split, P("batch", "win", None), split) + (P(),) * 10
    out_specs = (split, split) + (P(),) * 10
    return jax.shard_map(shards, mesh=mesh, in_specs=in_specs, out_specs=out_specs, check_vma=False)
```

time: 1160 us -> 572 us (0.49)
  waiting for transfers between devices: 424 us -> 138 us
  Pallas kernels: 0 us -> 282 us
  local copies, waits for them, and re-layouts: 338 us -> 69.3 us
  matrix products: 217 us -> 0 us
  other arithmetic: 121 us -> 53.1 us
  between operations: 16.7 us -> 1.54 us
    psum x4 -> x0, waiting for transfers between devices: 409 us -> none  [the longest x2 363 us: shards(): lax.psum((early_conv, early_gain, early_shift, grad_qkv_one, early_bias,...]
    pallas_call x0 -> x8, Pallas kernels: none -> 282 us  [the longest x1 62.3 us: shards(): call(stage_four, n, [per_image(wide), per_image(qkv_two.shape), per_image...]
    dot_general x35 -> x0, matrix products: 207 us -> none  [the longest x8 77.1 us: linear(): jnp.dot(inputs_b, weight, preferred_element_type=jnp.float32) + offset]
    ppermute x12 -> x18, waiting for transfers between devices: 14.4 us -> 138 us  [the longest x10 115 us: trade(): return lax.ppermute(value, ('batch', 'win'), pairs)]
    concatenate x9 -> x1, local copies, waits for them, and re-layouts: 67.7 us -> 0.67 us  [shards(): jnp.concatenate([pack_four, pack_five, pack_six, pack_seven, small], axis=0)]
    reduce_sum x21 -> x0, other arithmetic: 57 us -> none  [the longest x5 19.1 us: layer_norm(): center = volume - jnp.mean(volume, axis=-1, keepdims=True)]
    reshape x14 -> x2, local copies, waits for them, and re-layouts: 56.8 us -> 1.91 us  [the longest x1 1.87 us: shards(): jnp.pad(valid_mask.astype(F32), ((0, 0), (0, 0), (0, WIDE - COLS)))]
    convert_element_type x18 -> x8, local copies, waits for them, and re-layouts: 53.2 us -> 8.34 us  [untile(): return block.transpose(1, 0, 2).reshape(height, width).astype(F32)]
  transfers between devices with their start and end apart: 16 -> 18, of which waited for: 11 -> 16; matrix products, arithmetic and copies ran while one was open for 6% -> 4% of each run, Pallas kernels for 0% -> 1%
where the time goes in v1:
time: 572 us; the launch traced here: 562 us
  Pallas kernels  282 us (49%)
  waiting for transfers between devices  138 us (24%)
  local copies, waits for them, and re-layouts  69.3 us (12%)
  other arithmetic  53.1 us (9%)
  starting transfers between devices  18.2 us (3%)
    ppermute x10, waiting for transfers between devices, trade(): return lax.ppermute(value, ('batch', 'win'), pairs)  115 us
    pallas_call x1, Pallas kernels, shards(): call(stage_four, n, [per_image(wide), per_image(qkv_two.shape), per_image...  62.3 us
    pallas_call x1, Pallas kernels, shards(): call(stage_seven, n, [scalar(), per_image(wide), per_image(border), per_i...  58.4 us
    unnamed x91, local copies, waits for them, and re-layouts  50.2 us
    pallas_call x1, Pallas kernels, shards(): call(stage_six, n, [scalar(), per_image(wide), per_image(border), per_ima...  39.6 us
    pallas_call x1, Pallas kernels, shards(): call(stage_one, n, [scalar(), per_image(images.shape), per_image(img_halo...  38.1 us
    pallas_call x1, Pallas kernels, shards(): call(stage_two, n, [scalar(), per_image(wide), per_image(border), *small_...  31.7 us
    pallas_call x1, Pallas kernels, shards(): call(stage_five, n, [scalar(), per_image(wide), per_image(wide), per_imag...  26.1 us
  transfers between devices with their start and end apart: 18, of which 16 were waited for; matrix products, arithmetic and copies ran while one was open for 4% of the time, Pallas kernels for 1%

profile of v1, /device:TPU:0, one launch (start us, length us, event | category | flops | bytes accessed | tf_op | source)
XLA Modules:
  0.0 562.3 jit_solution(16699699353626786696)
XLA Ops:
  1.7 3.0 collective-permute-start
  8.6 38.1 %window_forward.1 = (f32[4,14,32,384]{3,2,1,0:T(8,128)}, bf16[4,512,384]{2,1,0:T(8,128)(2,1)}, bf16[4,512,1152]{2,1,0:T(8,128)(2,1)}, f32[4,512,768]{2,1,0:T(8,1...) custom-call(s32[1]{0:T(128)} %bitcast.side_ref, ...), custom_call_target="tpu_custom_call" | custom-call | flops 2000000000 | bytes 20000000 | tf_op jit(solution)/shard_map/window_forward/pallas_call | solution.py:687
  48.2 5.2 collective-permute-done.1.halo_ref
  54.0 31.7 %mlp_one_forward.1 = (f32[4,14,32,384]{3,2,1,0:T(8,128)}, bf16[4,448,384]{2,1,0:T(8,128)(2,1)}, bf16[4,448,1536]{2,1,0:T(8,128)(2,1)}, bf16[4,448,1536]{2,1,0:T(...) custom-call(s32[1]{0:T(128)} %bitcast.side_ref, f32[4,14,32,384]{3,2,1,0:T(8,128)} %get-tuple-element.47.x_ref, ...), custom_call_target="tpu_custom_call" | custom-call | flops 4000000000 | bytes 20000000 | tf_op jit(solution)/shard_map/mlp_one_forward/pallas_call | solution.py:697
  88.4 3.3 collective-permute-done.2.halo_ref
  92.4 20.2 %channel_gram.1 = (f32[4,14,32,384]{3,2,1,0:T(8,128)}, bf16[4,448,384]{2,1,0:T(8,128)(2,1)}, bf16[4,448,1152]{2,1,0:T(8,128)(2,1)}, f32[4,96,128]{2,1,0:T(8,128)}) custom-call(s32[1]{0:T(128)} %bitcast.side_ref, f32[4,14,32,384]{3,2,1,0:T(8,128)} %get-tuple-element.49.x_ref, f32[4,32,384]{2,1,0:T(8,128)} %copy-done.35, f32[3,10,384]{2,1,0:T(8,128)} %copy.57.conv_ref, ...), custom_call_target="tpu_custom_call" | custom-call | flops 2000000000 | bytes 20000000 | tf_op jit(solution)/shard_map/channel_gram/pallas_call | solution.py:708
  114.6 3.9 collective-permute-done.3.gram_b
  119.2 62.3 %mlp_two.1 = (f32[4,14,28,384]{3,2,1,0:T(8,128)}, f32[4,14,32,384]{3,2,1,0:T(8,128)}, bf16[4,448,384]{2,1,0:T(8,128)(2,1)}, f32[4,96,128]{2,1,0:T(8,128)}, bf16[10368,128]{1,0:T(8,128)(2,1)}, /*index=5*/f32[8,384]{1,0:T(8,128)}) custom-call(f32[4,14,32,384]{3,2,1,0:T(8,128)} %get-tuple-element.51.pos_ref, bf16[4,448,1152]{2,1,0:T(8,128)(2,1)} %get-tuple-element.52.qkv_ref, ...), custom_call_target="tpu_custom_call" | custom-call | flops 12000000000 | bytes 20000000 | tf_op jit(solution)/shard_map/mlp_two/pallas_call | solution.py:720
  182.2 2.9 constant_dynamic-update-slice_fusion.3
  188.1 26.1 %channel_backward.1 = (f32[4,14,32,384]{3,2,1,0:T(8,128)}, f32[4,32,384]{2,1,0:T(8,128)}, bf16[3456,128]{1,0:T(8,128)(2,1)}, f32[8,384]{1,0:T(8,128)}) custom-call(s32[1]{0:T(128)} %bitcast.side_ref, f32[4,14,32,384]{3,2,1,0:T(8,128)} %get-tuple-element.55.gres_ref, f32[4,14,32,384]{3,2,1,0:T(8,128)} %get-tuple-element.51.pos_ref, ...), custom_call_target="tpu_custom_call" | custom-call | flops 3000000000 | bytes 20000000 | tf_op jit(solution)/shard_map/channel_backward/pallas_call | solution.py:734
  220.9 39.6 %mlp_one_backward.1 = (f32[4,14,32,384]{3,2,1,0:T(8,128)}, f32[4,32,384]{2,1,0:T(8,128)}, bf16[9216,128]{1,0:T(8,128)(2,1)}, f32[24,384]{1,0:T(8,128)}) custom-call(s32[1]{0:T(128)} %bitcast.side_ref, f32[4,14,32,384]{3,2,1,0:T(8,128)} %get-tuple-element.59.g_ref, f32[4,32,384]{2,1,0:T(8,128)} %copy-done.34, f32[4,14,32,384]{3,2,1,0:T(8,128)} %get-tuple-element.49.x_ref, ...), custom_call_target="tpu_custom_call" | custom-call | flops 8000000000 | bytes 20000000 | tf_op jit(solution)/shard_map/mlp_one_backward/pallas_call | solution.py:745
  267.1 58.4 %window_backward.1 = (f32[4,14,32,384]{3,2,1,0:T(8,128)}, f32[4,32,384]{2,1,0:T(8,128)}, bf16[4608,128]{1,0:T(8,128)(2,1)}, f32[32,384]{1,0:T(8,128)}) custom-call(s32[1]{0:T(128)} %bitcast.side_ref, f32[4,14,32,384]{3,2,1,0:T(8,128)} %get-tuple-element.65.g_ref, f32[4,32,384]{2,1,0:T(8,128)} %copy-done.11, f32[4,14,32,384]{3,2,1,0:T(8,128)} %get-tuple-element.47.x_ref, ...), custom_call_target="tpu_custom_call" | custom-call | flops 5000000000 | bytes 20000000 | tf_op jit(solution)/shard_map/window_backward/pallas_call | solution.py:755
  329.4 3.4 constant_dynamic-slice_fusion.4
  332.8 6.7 %collective-permute-done.8 = bf16[14080,128]{1,0:T(8,128)(2,1)} collective-permute-done((bf16[14080,128]{1,0:T(8,128)(2,1)}, bf16[14080,128]{1,0:T(8,128)(2,1)}, u32[]{:S(2)}, u32[]{:S(2)}) %collective-permute-start.8) | collective-permute-done | bytes 3604512 | tf_op jit(solution)/shard_map/ppermute | solution.py:807
  339.5 4.0 add_convert_fusion
  346.2 22.3 %collective-permute-done.9 = bf16[7040,128]{1,0:T(8,128)(2,1)} collective-permute-done((bf16[7040,128]{1,0:T(8,128)(2,1)S(1)}, bf16[7040,128]{1,0:T(8,128)(2,1)}, u32[]{:S(2)}, u32[]{:S(2)}) %collective-permute-start.9) | collective-permute-done | bytes 1802272 | tf_op jit(solution)/shard_map/ppermute | solution.py:807
  372.6 11.8 %collective-permute-done.10 = bf16[3520,128]{1,0:T(8,128)(2,1)} collective-permute-done((bf16[3520,128]{1,0:T(8,128)(2,1)S(1)}, bf16[3520,128]{1,0:T(8,128)(2,1)}, u32[]{:S(2)}, u32[]{:S(2)}) %collective-permute-start.10) | collective-permute-done | bytes 901152 | tf_op jit(solution)/shard_map/ppermute | solution.py:807
  387.5 9.1 %collective-permute-done.11 = bf16[1760,128]{1,0:T(8,128)(2,1)S(1)} collective-permute-done((bf16[1760,128]{1,0:T(8,128)(2,1)S(1)}, bf16[1760,128]{1,0:T(8,128)(2,1)S(1)}, u32[]{:S(2)}, u32[]{:S(2)}) %collective-permute-start.11) | collective-permute-done | bytes 450592 | tf_op jit(solution)/shard_map/ppermute | solution.py:807
  399.5 8.1 %collective-permute-done.12 = bf16[880,128]{1,0:T(8,128)(2,1)S(1)} collective-permute-done((bf16[880,128]{1,0:T(8,128)(2,1)S(1)}, bf16[880,128]{1,0:T(8,128)(2,1)S(1)}, u32[]{:S(2)}, u32[]{:S(2)}) %collective-permute-start.12) | collective-permute-done | bytes 225312 | tf_op jit(solution)/shard_map/ppermute | solution.py:807
  407.7 12.1 %collective-permute-done.13 = bf16[880,128]{1,0:T(8,128)(2,1)S(1)} collective-permute-done((bf16[880,128]{1,0:T(8,128)(2,1)S(1)}, bf16[880,128]{1,0:T(8,128)(2,1)S(1)}, u32[]{:S(2)}, u32[]{:S(2)}) %collective-permute-start.13) | collective-permute-done | bytes 225312 | tf_op jit(solution)/shard_map/ppermute | solution.py:807
  419.9 11.4 %collective-permute-done.14 = bf16[1760,128]{1,0:T(8,128)(2,1)S(1)} collective-permute-done((bf16[1760,128]{1,0:T(8,128)(2,1)S(1)}, bf16[1760,128]{1,0:T(8,128)(2,1)S(1)}, u32[]{:S(2)}, u32[]{:S(2)}) %collective-permute-start.14) | collective-permute-done | bytes 450592 | tf_op jit(solution)/shard_map/ppermute | solution.py:807
  433.1 11.7 %collective-permute-done.15 = bf16[3520,128]{1,0:T(8,128)(2,1)S(1)} collective-permute-done((bf16[3520,128]{1,0:T(8,128)(2,1)S(1)}, bf16[3520,128]{1,0:T(8,128)(2,1)S(1)}, u32[]{:S(2)}, u32[]{:S(2)}) %collective-permute-start.15) | collective-permute-done | bytes 901152 | tf_op jit(solution)/shard_map/ppermute | solution.py:807
  447.2 22.3 %collective-permute-done.16 = bf16[7040,128]{1,0:T(8,128)(2,1)} collective-permute-done((bf16[7040,128]{1,0:T(8,128)(2,1)S(1)}, bf16[7040,128]{1,0:T(8,128)(2,1)}, u32[]{:S(2)}, u32[]{:S(2)}) %collective-permute-start.16) | collective-permute-done | bytes 1802272 | tf_op jit(solution)/shard_map/ppermute | solution.py:807
  472.1 13.9 %pad_maximum_fusion = bf16[14080,128]{1,0:T(8,128)(2,1)} fusion(bf16[7040,128]{1,0:T(8,128)(2,1)S(1)} %get-tuple-element.113, bf16[7040,128]{1,0:T(8,128)(2,1)S(1)} %get-tuple-element.112), kind=kLoop, calls=%fused_computation.1 | loop fusion | flops 7208960 | bytes 7208960 | tf_op jit(solution)/shard_map/concatenate | solution.py:824
  486.9 3.0 copy.76
  489.9 3.5 collective-permute-done.7.halo_ref
  494.2 5.5 images_backward.1
  499.7 4.8 copy.77
  504.4 14.0 %broadcast_select_fusion = (bf16[14080,128]{1,0:T(8,128)(2,1)S(1)}, bf16[14080,128]{1,0:T(8,128)(2,1)S(1)}) fusion(bf16[14080,128]{1,0:T(8,128)(2,1)} %collective-permute-done.17, pred[]{:T(512)S(6)} %eq.37, bf16[7040,128]{1,0:T(8,128)(2,1)S(1)} %get-tuple-element.113, bf16[7040,128]{1,0:T(8,128)(2,1)S(1)} %get-tuple-element.112), kind=kLoop, calls=%fused_computation.3 | loop fusion | flops 10813440 | bytes 14417921 | tf_op jit(solution)/shard_map/jit(_where)/select_n | solution.py:824
  529.8 3.2 copy.79
  542.2 6.1 %copy.81 = f32[2,384,1536]{2,1,0:T(8,128)} copy(f32[2,384,1536]{1,2,0:T(8,128)} %maximum_convert_fusion) | data formatting | bytes 9437184
  552.8 6.1 %copy.82 = f32[2,1536,384]{2,1,0:T(8,128)} copy(f32[2,1536,384]{1,2,0:T(8,128)} %maximum_convert_fusion.1) | data formatting | bytes 9437184
  (174 shorter events, 83.3 us)
Async XLA Ops:
  0.6 6.7 %copy-start.15 = (f32[3,10,384]{2,0,1:T(4,128)S(1)}, f32[3,10,384]{2,0,1:T(4,128)}, u32[]{:S(2)}) copy-start(f32[3,10,384]{2,0,1:T(4,128)} %param.20) | copy-start | bytes 138244
  1.7 6.2 %collective-permute-start = (bf16[4,28,384]{2,1,0:T(8,128)(2,1)S(1)}, bf16[4,28,384]{2,1,0:T(8,128)(2,1)S(1)}, u32[]{:S(2)}, u32[]{:S(2)}) collective-permute-start(bf16[4,28,384]{2,1,0:T(8,128)(2,1)S(1)} %fusion), channel_id=1, source_target_pairs={{0,1},{1,0},{2,3},{3,2},{4,5},{5,4},{6,7},{7,6},{8,9},{9,8},{10,11... | collective-permute-start | bytes 258056 | tf_op jit(solution)/shard_map/ppermute | solution.py:665
  46.7 6.7 %collective-permute-start.1 = (f32[4,32,384]{2,1,0:T(8,128)}, f32[4,32,384]{2,1,0:T(8,128)S(1)}, u32[]{:S(2)}, u32[]{:S(2)}) collective-permute-start(f32[4,32,384]{2,1,0:T(8,128)} %get-tuple-element.48), channel_id=1, source_target_pairs={{0,1},{1,0},{2,3},{3,2},{4,5},{5,4},{6,7},{7,6},{8,9},{9,8},{10,11... | collective-permute-start | bytes 589832 | tf_op jit(solution)/shard_map/ppermute | solution.py:665
  54.0 32.5 %copy-start.18 = (s32[4,14,28]{2,0,1:T(4,128)S(1)}, s32[4,14,28]{2,0,1:T(4,128)}, u32[]{:S(2)}) copy-start(s32[4,14,28]{2,0,1:T(4,128)} %param.18) | copy-start | bytes 18820
  85.7 5.9 %collective-permute-start.2 = (f32[4,32,384]{2,1,0:T(8,128)}, f32[4,32,384]{2,1,0:T(8,128)S(1)}, u32[]{:S(2)}, u32[]{:S(2)}) collective-permute-start(f32[4,32,384]{2,1,0:T(8,128)} %get-tuple-element.50), channel_id=1, source_target_pairs={{0,1},{1,0},{2,3},{3,2},{4,5},{5,4},{6,7},{7,6},{8,9},{9,8},{10,11... | collective-permute-start | bytes 589832 | tf_op jit(solution)/shard_map/ppermute | solution.py:665
  92.4 20.9 %copy-start.8 = (bf16[4,14,28,384]{3,0,2,1:T(4,128)(2,1)S(1)}, bf16[4,14,28,384]{3,0,2,1:T(4,128)(2,1)}, u32[]{:S(2)}) copy-start(bf16[4,14,28,384]{3,0,2,1:T(4,128)(2,1)} %param.19) | copy-start | bytes 3612676
  112.6 5.9 %collective-permute-start.3 = (f32[4,96,128]{2,1,0:T(8,128)}, f32[4,96,128]{2,1,0:T(8,128)S(1)}, u32[]{:S(2)}, u32[]{:S(2)}) collective-permute-start(f32[4,96,128]{2,1,0:T(8,128)} %get-tuple-element.53.gram_a), channel_id=1, source_target_pairs={{0,1},{1,0},{2,3},{3,2},{4,5},{5,4},{6,7},{7,6},{8,9},{9,8},{10,11... | collective-permute-start | bytes 589832 | tf_op jit(solution)/shard_map/ppermute | solution.py:665
  181.5 5.9 %collective-permute-start.4 = (f32[4,96,128]{2,1,0:T(8,128)}, f32[4,96,128]{2,1,0:T(8,128)S(1)}, u32[]{:S(2)}, u32[]{:S(2)}) collective-permute-start(f32[4,96,128]{2,1,0:T(8,128)} %get-tuple-element.58.gchan_a), channel_id=1, source_target_pairs={{0,1},{1,0},{2,3},{3,2},{4,5},{5,4},{6,7},{7,6},{8,9},{9,8},{10,11... | collective-permute-start | bytes 589832 | tf_op jit(solution)/shard_map/ppermute | solution.py:665
  214.2 5.9 %collective-permute-start.5 = (f32[4,32,384]{2,1,0:T(8,128)}, f32[4,32,384]{2,1,0:T(8,128)S(1)}, u32[]{:S(2)}, u32[]{:S(2)}) collective-permute-start(f32[4,32,384]{2,1,0:T(8,128)} %get-tuple-element.60), channel_id=1, source_target_pairs={{0,1},{1,0},{2,3},{3,2},{4,5},{5,4},{6,7},{7,6},{8,9},{9,8},{10,11... | collective-permute-start | bytes 589832 | tf_op jit(solution)/shard_map/ppermute | solution.py:665
  260.4 5.9 %collective-permute-start.6 = (f32[4,32,384]{2,1,0:T(8,128)}, f32[4,32,384]{2,1,0:T(8,128)S(1)}, u32[]{:S(2)}, u32[]{:S(2)}) collective-permute-start(f32[4,32,384]{2,1,0:T(8,128)} %get-tuple-element.66), channel_id=1, source_target_pairs={{0,1},{1,0},{2,3},{3,2},{4,5},{5,4},{6,7},{7,6},{8,9},{9,8},{10,11... | collective-permute-start | bytes 589832 | tf_op jit(solution)/shard_map/ppermute | solution.py:665
  332.8 6.7 %collective-permute-start.8 = (bf16[14080,128]{1,0:T(8,128)(2,1)}, bf16[14080,128]{1,0:T(8,128)(2,1)}, u32[]{:S(2)}, u32[]{:S(2)}) collective-permute-start(bf16[14080,128]{1,0:T(8,128)(2,1)} %constant_dynamic-slice_fusion.4), channel_id=1, source_target_pairs={{0,2},{1,3},{2,0},{3,1},{4,6},{5,7},{6,4},{7,5},{8,10},{9,11},{10,... | collective-permute-start | bytes 10813448 | tf_op jit(solution)/shard_map/ppermute | solution.py:807
  345.4 23.0 %collective-permute-start.9 = (bf16[7040,128]{1,0:T(8,128)(2,1)S(1)}, bf16[7040,128]{1,0:T(8,128)(2,1)}, u32[]{:S(2)}, u32[]{:S(2)}) collective-permute-start(bf16[7040,128]{1,0:T(8,128)(2,1)S(1)} %constant_dynamic-slice_fusion.3), channel_id=1, source_target_pairs={{0,1},{1,0},{2,6},{3,7},{4,5},{5,4},{6,2},{7,3},{8,9},{9,8},{10,14... | collective-permute-start | bytes 5406728 | tf_op jit(solution)/shard_map/ppermute | solution.py:807
  371.1 13.4 %collective-permute-start.10 = (bf16[3520,128]{1,0:T(8,128)(2,1)S(1)}, bf16[3520,128]{1,0:T(8,128)(2,1)}, u32[]{:S(2)}, u32[]{:S(2)}) collective-permute-start(bf16[3520,128]{1,0:T(8,128)(2,1)S(1)} %constant_dynamic-slice_fusion.2), channel_id=1, source_target_pairs={{0,4},{1,5},{2,3},{3,2},{4,0},{5,1},{6,7},{7,6},{8,12},{9,13},{10,... | collective-permute-start | bytes 2703368 | tf_op jit(solution)/shard_map/ppermute | solution.py:807
  385.9 10.7 %collective-permute-start.11 = (bf16[1760,128]{1,0:T(8,128)(2,1)S(1)}, bf16[1760,128]{1,0:T(8,128)(2,1)S(1)}, u32[]{:S(2)}, u32[]{:S(2)}) collective-permute-start(bf16[1760,128]{1,0:T(8,128)(2,1)S(1)} %constant_dynamic-slice_fusion.1), channel_id=1, source_target_pairs={{0,8},{1,9},{2,10},{3,11},{4,12},{5,13},{6,14},{7,15},{8,0},{9,1},... | collective-permute-start | bytes 1351688 | tf_op jit(solution)/shard_map/ppermute | solution.py:807
  396.8 10.7 %collective-permute-start.12 = (bf16[880,128]{1,0:T(8,128)(2,1)S(1)}, bf16[880,128]{1,0:T(8,128)(2,1)S(1)}, u32[]{:S(2)}, u32[]{:S(2)}) collective-permute-start(bf16[880,128]{1,0:T(8,128)(2,1)S(1)} %constant_dynamic-slice_fusion), channel_id=1, source_target_pairs={{0,16},{1,17},{2,18},{3,19},{4,20},{5,21},{6,22},{7,23},{8,24},{9,... | collective-permute-start | bytes 675848 | tf_op jit(solution)/shard_map/ppermute | solution.py:807
  407.6 12.2 %collective-permute-start.13 = (bf16[880,128]{1,0:T(8,128)(2,1)S(1)}, bf16[880,128]{1,0:T(8,128)(2,1)S(1)}, u32[]{:S(2)}, u32[]{:S(2)}) collective-permute-start(bf16[880,128]{1,0:T(8,128)(2,1)S(1)} %add_convert_fusion.4), channel_id=1, source_target_pairs={{0,16},{1,17},{2,18},{3,19},{4,20},{5,21},{6,22},{7,23},{8,24},{9,... | collective-permute-start | bytes 675848 | tf_op jit(solution)/shard_map/ppermute | solution.py:807
  419.8 11.5 %collective-permute-start.14 = (bf16[1760,128]{1,0:T(8,128)(2,1)S(1)}, bf16[1760,128]{1,0:T(8,128)(2,1)S(1)}, u32[]{:S(2)}, u32[]{:S(2)}) collective-permute-start(bf16[1760,128]{1,0:T(8,128)(2,1)S(1)} %pad_maximum_fusion.4), channel_id=1, source_target_pairs={{0,8},{1,9},{2,10},{3,11},{4,12},{5,13},{6,14},{7,15},{8,0},{9,1},... | collective-permute-start | bytes 1351688 | tf_op jit(solution)/shard_map/ppermute | solution.py:807
  431.5 13.3 %collective-permute-start.15 = (bf16[3520,128]{1,0:T(8,128)(2,1)S(1)}, bf16[3520,128]{1,0:T(8,128)(2,1)S(1)}, u32[]{:S(2)}, u32[]{:S(2)}) collective-permute-start(bf16[3520,128]{1,0:T(8,128)(2,1)S(1)} %pad_maximum_fusion.3), channel_id=1, source_target_pairs={{0,4},{1,5},{2,3},{3,2},{4,0},{5,1},{6,7},{7,6},{8,12},{9,13},{10,... | collective-permute-start | bytes 2703368 | tf_op jit(solution)/shard_map/ppermute | solution.py:807
  446.5 23.0 %collective-permute-start.16 = (bf16[7040,128]{1,0:T(8,128)(2,1)S(1)}, bf16[7040,128]{1,0:T(8,128)(2,1)}, u32[]{:S(2)}, u32[]{:S(2)}) collective-permute-start(bf16[7040,128]{1,0:T(8,128)(2,1)S(1)} %pad_maximum_fusion.1), channel_id=1, source_target_pairs={{0,1},{1,0},{2,6},{3,7},{4,5},{5,4},{6,2},{7,3},{8,9},{9,8},{10,14... | collective-permute-start | bytes 5406728 | tf_op jit(solution)/shard_map/ppermute | solution.py:807
  472.1 14.0 %copy-start.33 = (f32[4,32,384]{2,1,0:T(8,128)S(1)}, f32[4,32,384]{2,1,0:T(8,128)}, u32[]{:S(2)}) copy-start(f32[4,32,384]{2,1,0:T(8,128)} %get-tuple-element.73) | copy-start | bytes 589828
  472.1 14.8 %copy-start.7 = (f32[4,14,28,384]{3,2,1,0:T(8,128)S(1)}, f32[4,14,28,384]{3,2,1,0:T(8,128)}, u32[]{:S(2)}) copy-start(f32[4,14,28,384]{3,2,1,0:T(8,128)} %get-tuple-element.94) | copy-start | bytes 7225348
  486.1 18.4 %collective-permute-start.17 = (bf16[14080,128]{1,0:T(8,128)(2,1)}, bf16[14080,128]{1,0:T(8,128)(2,1)}, u32[]{:S(2)}, u32[]{:S(2)}) collective-permute-start(bf16[14080,128]{1,0:T(8,128)(2,1)} %pad_maximum_fusion), channel_id=1, source_target_pairs={{0,2},{1,3},{2,0},{3,1},{4,6},{5,7},{6,4},{7,5},{8,10},{9,11},{10,... | collective-permute-start | bytes 10813448 | tf_op jit(solution)/shard_map/ppermute | solution.py:807
  486.2 7.3 %collective-permute-start.7 = (f32[4,32,384]{2,1,0:T(8,128)S(1)}, f32[4,32,384]{2,1,0:T(8,128)S(1)}, u32[]{:S(2)}, u32[]{:S(2)}) collective-permute-start(f32[4,32,384]{2,1,0:T(8,128)S(1)} %copy-done.33), channel_id=1, source_target_pairs={{0,1},{1,0},{2,3},{3,2},{4,5},{5,4},{6,7},{7,6},{8,9},{9,8},{10,11... | collective-permute-start | bytes 589832 | tf_op jit(solution)/shard_map/ppermute | solution.py:665
  552.7 6.2 %copy-start.27 = (f32[1,1,3,128]{3,2,1,0:T(4,128)S(1)}, f32[1,1,3,128]{3,2,1,0:T(4,128)}, u32[]{:S(2)}) copy-start(f32[1,1,3,128]{3,2,1,0:T(4,128)} %get-tuple-element.126) | copy-start | bytes 4612
  552.8 6.2 %copy-start.25 = (f32[1,1,3,128]{3,2,1,0:T(4,128)S(1)}, f32[1,1,3,128]{3,2,1,0:T(4,128)}, u32[]{:S(2)}) copy-start(f32[1,1,3,128]{3,2,1,0:T(4,128)} %get-tuple-element.128) | copy-start | bytes 4612
  552.8 6.2 %copy-start.26 = (f32[1,1,3,128]{3,2,1,0:T(4,128)S(1)}, f32[1,1,3,128]{3,2,1,0:T(4,128)}, u32[]{:S(2)}) copy-start(f32[1,1,3,128]{3,2,1,0:T(4,128)} %get-tuple-element.129) | copy-start | bytes 4612
  552.8 6.2 %copy-start.23 = (f32[1,1,3,128]{3,2,1,0:T(4,128)S(1)}, f32[1,1,3,128]{3,2,1,0:T(4,128)}, u32[]{:S(2)}) copy-start(f32[1,1,3,128]{3,2,1,0:T(4,128)} %get-tuple-element.124) | copy-start | bytes 4612
  552.8 6.2 %copy-start.24 = (f32[1,1,3,128]{3,2,1,0:T(4,128)S(1)}, f32[1,1,3,128]{3,2,1,0:T(4,128)}, u32[]{:S(2)}) copy-start(f32[1,1,3,128]{3,2,1,0:T(4,128)} %get-tuple-element.125) | copy-start | bytes 4612
  552.8 6.3 %copy-start.17 = (f32[1,1,12,128]{3,2,1,0:T(8,128)S(1)}, f32[1,1,12,128]{3,2,1,0:T(8,128)}, u32[]{:S(2)}) copy-start(f32[1,1,12,128]{3,2,1,0:T(8,128)} %get-tuple-element.135) | copy-start | bytes 18436
  552.8 6.9 %copy-start.21 = (f32[1,1,3,128]{3,2,1,0:T(4,128)S(1)}, f32[1,1,3,128]{3,2,1,0:T(4,128)}, u32[]{:S(2)}) copy-start(f32[1,1,3,128]{3,2,1,0:T(4,128)} %get-tuple-element.122) | copy-start | bytes 4612
  552.8 6.9 %copy-start.22 = (f32[1,1,3,128]{3,2,1,0:T(4,128)S(1)}, f32[1,1,3,128]{3,2,1,0:T(4,128)}, u32[]{:S(2)}) copy-start(f32[1,1,3,128]{3,2,1,0:T(4,128)} %get-tuple-element.123) | copy-start | bytes 4612
  552.8 8.7 %copy-start.19 = (f32[3,384]{1,0:T(4,128)S(1)}, f32[3,384]{1,0:T(4,128)}, u32[]{:S(2)}) copy-start(f32[3,384]{1,0:T(4,128)} %slice.197) | copy-start | bytes 13828
  (24 other events, 67.4 us)
